TPU v7x, 512 devices: a whole 4x4x16 slice. The times are simulated.
512 devices in a mesh: member: 16 (over z), band: 32 (over y, x, core).
Axes of the slice: x: 4, y: 4, z: 16, core: 2. Of those that a mesh axis runs over, the one named last changes fastest.
Arguments:
- codes: int32 [64, 384, 6, 1408], P('member', 'band'), may hold values from -127 to 127
- exponents: int32 [64, 384, 6], P('member', 'band'), may hold values from -8 to -4
- centers: float32 [6, 256], replicated, may hold values from -3 to 3
- widths: float32 [6], replicated, may hold values from 0.01 to 0.03
Outputs:
- smoothed: bfloat16 [384, 6, 1408, 256], P('band', None, 'member')
All inputs are finite; a program needn't handle non-finite values.
Results may differ from a plain program's by a relative error of at most 0.0034.
Values may be sent and summed in bfloat16 or wider, within the bound.
No kernel may reach another device: no remote copies, remote signals or barrier semaphores. Data moves between devices by JAX's collectives and lax.ppermute only.
A program may use at most 64 MiB of HBM per device.

v0:
```python
import math

import jax
import jax.numpy as jnp
from jax import lax
from jax.sharding import PartitionSpec as P


def cut_along(array, dim, length):
    before, after = (array.shape[:dim], array.shape[dim + 1 :])
    return jnp.moveaxis(array.reshape(*before, length, -1, *after), dim, 0)


def edges_of(length, count):
    unit = 8 if length >= 8 * count else 1
    return [length // unit * k // count * unit for k in range(1, count)]


def joined_along(tiles, dim):
    dims = list(tiles.shape[1:])
    dims[dim] *= tiles.shape[0]
    return jnp.moveaxis(tiles, 0, dim).reshape(dims)


def cut_exchange(array, axis, pieces, split_dim, concat_dim):
    tiles = cut_along(array, split_dim, lax.axis_size(axis))
    widest = max(range(1, max(2, tiles.ndim - 1)), key=lambda d: tiles.shape[d])
    finished = []
    for slab in jnp.split(tiles, edges_of(tiles.shape[widest], pieces), axis=widest):
        if slab.size:
            finished.append(lax.all_to_all(slab, axis, split_axis=0, concat_axis=0, tiled=True))
    return joined_along(jnp.concatenate(finished, axis=widest), concat_dim)


def extended(cells, sides, width):
    for axis, dim in sides:
        count = lax.axis_size(axis)
        ends = count - 1
        head = lax.slice_in_dim(cells, 0, width, axis=dim)
        tail = lax.slice_in_dim(cells, cells.shape[dim] - width, cells.shape[dim], axis=dim)
        cells = jnp.concatenate(
            [
                lax.ppermute(tail, axis, [(i, (i + 1) % count) for i in range(ends)]),
                cells,
                lax.ppermute(head, axis, [((i + 1) % count, i) for i in range(ends)]),
            ],
            axis=dim,
        )
    return cells


def var_density(item, center, width):
    field = item.astype(jnp.float32)
    scaled = (center[None, None, None, :] - field[:, :, :, None]) / width
    total = jnp.sum(jnp.exp(-0.5 * scaled * scaled), axis=0)
    return total / (field.shape[0] * width * math.sqrt(2.0 * math.pi))


def block_density(values, centers, widths):
    items = jnp.transpose(values, (2, 0, 1, 3))
    dens = lax.map(lambda t: var_density(t[0], t[1], t[2]), (items, centers, widths))
    return jnp.transpose(dens, (1, 0, 2, 3)).astype(jnp.bfloat16)


def shards(codes, exponents, centers, widths):
    scale = jnp.exp2(exponents.astype(jnp.float32))
    values = (codes.astype(jnp.float32) * scale[..., None]).astype(jnp.bfloat16)
    owned = cut_exchange(values, "member", 2, 3, 0)
    rows = owned.shape[1]
    cells = owned.shape[3]
    dens = block_density(owned, centers, widths)
    padded = extended(dens, (("member", 2), ("band", 0)), 2)
    padded = padded.astype(jnp.float32)
    lat_sum = (
        padded[0:rows]
        + padded[1 : rows + 1]
        + padded[2 : rows + 2]
        + padded[3 : rows + 3]
        + padded[4 : rows + 4]
    )
    total = (
        lat_sum[:, :, 0:cells]
        + lat_sum[:, :, 1 : cells + 1]
        + lat_sum[:, :, 2 : cells + 2]
        + lat_sum[:, :, 3 : cells + 3]
        + lat_sum[:, :, 4 : cells + 4]
    )
    return (total / 25.0).astype(jnp.bfloat16)


def solution(mesh):
    return jax.shard_map(
        shards,
        mesh=mesh,
        in_specs=(P("member", "band", None, None), P("member", "band", None), P(), P()),
        out_specs=P("band", None, "member", None),
        check_vma=False,
    )
```

profile of v0, /device:TPU:7, one launch (start us, length us, event | category | flops | bytes accessed | tf_op | source)
XLA Modules:
  0.0 280.7 jit_solution(13530440793026917644)
XLA Ops:
  0.0 0.7 multiply_exponential_fusion
  0.9 1.8 multiply_convert_fusion
  2.7 2.3 reshape.31
  5.2 1.0 copy.17
  6.3 14.9 %all-to-all-start = ((bf16[16,4,6,6,88]{4,1,3,2,0:T(4,128)(2,1)}), bf16[16,4,6,6,88]{4,1,3,2,0:T(4,128)(2,1)S(1)}, u32[]{:S(2)}, u32[]{:S(2)}) async-start(bf16[16,4,6,6,88]{4,1,3,2,0:T(4,128)(2,1)} %copy.17), calls=%async_computation | async-start | bytes 1179648 | tf_op jit(solution)/shard_map/all_to_all | solution.py:31
  21.2 1.0 copy.18
  22.2 24.3 %all-to-all-done = bf16[16,4,6,6,88]{4,1,3,2,0:T(4,128)(2,1)S(1)} async-done(((bf16[16,4,6,6,88]{4,1,3,2,0:T(4,128)(2,1)}), bf16[16,4,6,6,88]{4,1,3,2,0:T(4,128)(2,1)S(1)}, u32[]{:S(2)}, u32[]{:S(2)}) %all-to-all-start) | async-done | bytes 405536 | tf_op jit(solution)/shard_map/all_to_all | solution.py:31
  46.5 0.8 copy-done
  47.3 13.0 %all-to-all-start.1 = ((bf16[16,4,6,6,88]{4,1,3,2,0:T(4,128)(2,1)}), bf16[16,4,6,6,88]{4,1,3,2,0:T(4,128)(2,1)}, u32[]{:S(2)}, u32[]{:S(2)}) async-start(bf16[16,4,6,6,88]{4,1,3,2,0:T(4,128)(2,1)} %copy.18), calls=%async_computation.1 | async-start | bytes 1179648 | tf_op jit(solution)/shard_map/all_to_all | solution.py:31
  60.4 25.4 %all-to-all-done.1 = bf16[16,4,6,6,88]{4,1,3,2,0:T(4,128)(2,1)} async-done(((bf16[16,4,6,6,88]{4,1,3,2,0:T(4,128)(2,1)}), bf16[16,4,6,6,88]{4,1,3,2,0:T(4,128)(2,1)}, u32[]{:S(2)}, u32[]{:S(2)}) %all-to-all-start.1) | async-done | bytes 405536 | tf_op jit(solution)/shard_map/all_to_all | solution.py:31
  85.7 2.2 pad_maximum_fusion
  87.9 1.7 copy.19
  89.6 134.4 %while.12 = (s32[]{:T(128)}, bf16[6,12,88,256]{3,2,0,1:T(8,128)(2,1)S(1)}, f32[6,256]{1,0:T(8,128)}, bf16[6,64,12,88]{3,1,0,2:T(8,128)(2,1)}, f32[6]{0:T(128)S(1)}, /*index=5*/s32[]{:T(128)}, f32[]{:T(128)}) while((s32[]{:T(128)}, bf16[6,12,88,256]{3,2,0,1:T(8,128)(2,1)S(1)}, f32[6,256]{1,0:T(8,128)}, bf16[6,64,12,88]{3,1,0,2:T(8,128)(2,1)}, ...), condition=%wide.region_2.3_spmd, body=%wide.region_0.2_spmd.sunk | while | flops 86575104 | bytes 4193409 | solution.py:61
  89.6 0.6 dynamic_slice.28
  90.8 0.7 constant_dynamic-slice_fusion.5
  91.6 0.9 constant_dynamic-slice_fusion.4
  92.6 19.2 %fusion.10 = f32[12,88,256]{2,1,0:T(8,128)S(1)} fusion(f32[]{:T(128)} %bitcast.26, f32[64,12,88]{2,1,0:T(8,128)S(1)} %fusion.9, f32[256]{0:T(256)S(1)} %bitcast.33), kind=kLoop, calls=%fused_computation.2.clone.1 | loop fusion | flops 86237184 | bytes 1352708 | tf_op jit(solution)/shard_map/while/body/eval_jaxpr/reduce_sum | solution.py:55
  112.0 0.7 dynamic_slice.28
  113.2 0.7 constant_dynamic-slice_fusion.5
  114.0 0.9 constant_dynamic-slice_fusion.4
  115.0 19.2 %fusion.10 = f32[12,88,256]{2,1,0:T(8,128)S(1)} fusion(f32[]{:T(128)} %bitcast.26, f32[64,12,88]{2,1,0:T(8,128)S(1)} %fusion.9, f32[256]{0:T(256)S(1)} %bitcast.33), kind=kLoop, calls=%fused_computation.2.clone.1 | loop fusion | flops 86237184 | bytes 1352708 | tf_op jit(solution)/shard_map/while/body/eval_jaxpr/reduce_sum | solution.py:55
  134.4 0.7 dynamic_slice.28
  135.7 0.7 constant_dynamic-slice_fusion.5
  136.4 0.9 constant_dynamic-slice_fusion.4
  137.4 19.2 %fusion.10 = f32[12,88,256]{2,1,0:T(8,128)S(1)} fusion(f32[]{:T(128)} %bitcast.26, f32[64,12,88]{2,1,0:T(8,128)S(1)} %fusion.9, f32[256]{0:T(256)S(1)} %bitcast.33), kind=kLoop, calls=%fused_computation.2.clone.1 | loop fusion | flops 86237184 | bytes 1352708 | tf_op jit(solution)/shard_map/while/body/eval_jaxpr/reduce_sum | solution.py:55
  156.8 0.7 dynamic_slice.28
  158.1 0.7 constant_dynamic-slice_fusion.5
  158.8 0.9 constant_dynamic-slice_fusion.4
  159.8 19.2 %fusion.10 = f32[12,88,256]{2,1,0:T(8,128)S(1)} fusion(f32[]{:T(128)} %bitcast.26, f32[64,12,88]{2,1,0:T(8,128)S(1)} %fusion.9, f32[256]{0:T(256)S(1)} %bitcast.33), kind=kLoop, calls=%fused_computation.2.clone.1 | loop fusion | flops 86237184 | bytes 1352708 | tf_op jit(solution)/shard_map/while/body/eval_jaxpr/reduce_sum | solution.py:55
  179.2 0.7 dynamic_slice.28
  180.5 0.7 constant_dynamic-slice_fusion.5
  181.2 0.9 constant_dynamic-slice_fusion.4
  182.2 19.2 %fusion.10 = f32[12,88,256]{2,1,0:T(8,128)S(1)} fusion(f32[]{:T(128)} %bitcast.26, f32[64,12,88]{2,1,0:T(8,128)S(1)} %fusion.9, f32[256]{0:T(256)S(1)} %bitcast.33), kind=kLoop, calls=%fused_computation.2.clone.1 | loop fusion | flops 86237184 | bytes 1352708 | tf_op jit(solution)/shard_map/while/body/eval_jaxpr/reduce_sum | solution.py:55
  201.6 0.7 dynamic_slice.28
  202.9 0.7 constant_dynamic-slice_fusion.5
  203.6 0.9 constant_dynamic-slice_fusion.4
  204.6 19.2 %fusion.10 = f32[12,88,256]{2,1,0:T(8,128)S(1)} fusion(f32[]{:T(128)} %bitcast.26, f32[64,12,88]{2,1,0:T(8,128)S(1)} %fusion.9, f32[256]{0:T(256)S(1)} %bitcast.33), kind=kLoop, calls=%fused_computation.2.clone.1 | loop fusion | flops 86237184 | bytes 1352708 | tf_op jit(solution)/shard_map/while/body/eval_jaxpr/reduce_sum | solution.py:55
  224.1 5.2 %collective-permute-start = (bf16[12,6,2,256]{3,2,1,0:T(2,128)(2,1)S(1)}, bf16[12,6,2,256]{3,2,1,0:T(2,128)(2,1)S(1)}, u32[]{:S(2)}, u32[]{:S(2)}) collective-permute-start(bf16[12,6,2,256]{3,2,1,0:T(2,128)(2,1)S(1)} %get-tuple-element.93), channel_id=1, source_target_pairs={{0,32},{32,64},{64,96},{96,128},{128,160},{160,192},{192,224},{224... | collective-permute-start | bytes 221192 | tf_op jit(solution)/shard_map/ppermute | solution.py:43
  229.3 1.3 collective-permute-start.1
  230.7 3.7 %collective-permute-done.1 = bf16[12,6,2,256]{3,2,1,0:T(2,128)(2,1)S(1)} collective-permute-done((bf16[12,6,2,256]{3,2,1,0:T(2,128)(2,1)S(1)}, bf16[12,6,2,256]{3,2,1,0:T(2,128)(2,1)S(1)}, u32[]{:S(2)}, u32[]{:S(2)}) %collective-permute-start.1) | collective-permute-done | bytes 73760 | tf_op jit(solution)/shard_map/ppermute | solution.py:45
  234.4 0.7 pad_maximum_fusion.3
  235.2 9.9 %collective-permute-start.2 = (bf16[2,6,92,256]{3,2,1,0:T(8,128)(2,1)S(1)}, bf16[2,6,92,256]{3,2,1,0:T(8,128)(2,1)S(1)}, u32[]{:S(2)}, u32[]{:S(2)}) collective-permute-start(bf16[2,6,92,256]{3,2,1,0:T(8,128)(2,1)S(1)} %get-tuple-element.91), channel_id=1, source_target_pairs={{0,1},{1,2},{2,3},{3,4},{4,5},{5,6},{6,7},{7,8},{8,9},{9,10},{10,1... | collective-permute-start | bytes 1695752 | tf_op jit(solution)/shard_map/ppermute | solution.py:43
  245.0 1.9 collective-permute-start.3
  247.0 4.9 %collective-permute-done.2 = bf16[2,6,92,256]{3,2,1,0:T(8,128)(2,1)S(1)} collective-permute-done((bf16[2,6,92,256]{3,2,1,0:T(8,128)(2,1)S(1)}, bf16[2,6,92,256]{3,2,1,0:T(8,128)(2,1)S(1)}, u32[]{:S(2)}, u32[]{:S(2)}) %collective-permute-start.2) | collective-permute-done | bytes 565280 | tf_op jit(solution)/shard_map/ppermute | solution.py:43
  251.9 6.5 %collective-permute-done.3 = bf16[2,6,92,256]{3,2,1,0:T(8,128)(2,1)S(1)} collective-permute-done((bf16[2,6,92,256]{3,2,1,0:T(8,128)(2,1)S(1)}, bf16[2,6,92,256]{3,2,1,0:T(8,128)(2,1)S(1)}, u32[]{:S(2)}, u32[]{:S(2)}) %collective-permute-start.3) | collective-permute-done | bytes 565280 | tf_op jit(solution)/shard_map/ppermute | solution.py:45
  258.4 4.5 %maximum_convert_fusion = f32[16,6,92,256]{3,2,1,0:T(8,128)} fusion(bf16[2,6,92,256]{3,2,1,0:T(8,128)(2,1)S(1)} %collective-permute-done.3, bf16[12,6,2,256]{3,2,1,0:T(2,128)(2,1)S(1)} %collective-permute-done.1, bf16[12,6,88,256]{3,2,1,0:T(8,128)(2,1)S(1)} %bitcast.30, bf16[12,6,2,256]{3,2,1,0:T(2,128)(2,1)S(1)} %collective-permute-done, ...), kind=kLoop, calls=%fused_computation.18 | loop fusion | flops 22609920 | bytes 13565952 | tf_op jit(solution)/shard_map/convert_element_type | solution.py:73
  262.9 13.6 %slice_add_fusion = f32[12,6,92,256]{3,2,1,0:T(8,128)S(1)} fusion(f32[16,6,92,256]{3,2,1,0:T(8,128)} %maximum_convert_fusion), kind=kLoop, calls=%fused_computation.8 | loop fusion | flops 6782976 | bytes 40697856 | tf_op jit(solution)/shard_map/add | solution.py:75
  276.5 4.2 %fusion.4 = bf16[12,6,88,256]{3,2,1,0:T(8,128)(2,1)} fusion(f32[12,6,92,256]{3,2,1,0:T(8,128)S(1)} %slice_add_fusion), kind=kLoop, calls=%fused_computation.14 | loop fusion | flops 9732096 | bytes 35684352 | tf_op jit(solution)/shard_map/convert_element_type | solution.py:88
  (20 shorter events, 1.9 us)
Async XLA Ops:
  5.2 84.4 %copy-start.1 = (f32[6]{0:T(128)S(1)}, f32[6]{0:T(128)}, u32[]{:S(2)}) copy-start(f32[6]{0:T(128)} %param.9) | copy-start | bytes 76
  6.3 40.3 %all-to-all-start = ((bf16[16,4,6,6,88]{4,1,3,2,0:T(4,128)(2,1)}), bf16[16,4,6,6,88]{4,1,3,2,0:T(4,128)(2,1)S(1)}, u32[]{:S(2)}, u32[]{:S(2)}) async-start(bf16[16,4,6,6,88]{4,1,3,2,0:T(4,128)(2,1)} %copy.17), calls=%async_computation | async-start | bytes 1179648 | tf_op jit(solution)/shard_map/all_to_all | solution.py:31
  46.5 0.8 copy-start
  47.3 38.4 %all-to-all-start.1 = ((bf16[16,4,6,6,88]{4,1,3,2,0:T(4,128)(2,1)}), bf16[16,4,6,6,88]{4,1,3,2,0:T(4,128)(2,1)}, u32[]{:S(2)}, u32[]{:S(2)}) async-start(bf16[16,4,6,6,88]{4,1,3,2,0:T(4,128)(2,1)} %copy.18), calls=%async_computation.1 | async-start | bytes 1179648 | tf_op jit(solution)/shard_map/all_to_all | solution.py:31
  224.1 6.6 %collective-permute-start = (bf16[12,6,2,256]{3,2,1,0:T(2,128)(2,1)S(1)}, bf16[12,6,2,256]{3,2,1,0:T(2,128)(2,1)S(1)}, u32[]{:S(2)}, u32[]{:S(2)}) collective-permute-start(bf16[12,6,2,256]{3,2,1,0:T(2,128)(2,1)S(1)} %get-tuple-element.93), channel_id=1, source_target_pairs={{0,32},{32,64},{64,96},{96,128},{128,160},{160,192},{192,224},{224... | collective-permute-start | bytes 221192 | tf_op jit(solution)/shard_map/ppermute | solution.py:43
  229.3 5.1 %collective-permute-start.1 = (bf16[12,6,2,256]{3,2,1,0:T(2,128)(2,1)S(1)}, bf16[12,6,2,256]{3,2,1,0:T(2,128)(2,1)S(1)}, u32[]{:S(2)}, u32[]{:S(2)}) collective-permute-start(bf16[12,6,2,256]{3,2,1,0:T(2,128)(2,1)S(1)} %get-tuple-element.94), channel_id=1, source_target_pairs={{32,0},{64,32},{96,64},{128,96},{160,128},{192,160},{224,192},{256... | collective-permute-start | bytes 221192 | tf_op jit(solution)/shard_map/ppermute | solution.py:45
  235.2 16.7 %collective-permute-start.2 = (bf16[2,6,92,256]{3,2,1,0:T(8,128)(2,1)S(1)}, bf16[2,6,92,256]{3,2,1,0:T(8,128)(2,1)S(1)}, u32[]{:S(2)}, u32[]{:S(2)}) collective-permute-start(bf16[2,6,92,256]{3,2,1,0:T(8,128)(2,1)S(1)} %get-tuple-element.91), channel_id=1, source_target_pairs={{0,1},{1,2},{2,3},{3,4},{4,5},{5,6},{6,7},{7,8},{8,9},{9,10},{10,1... | collective-permute-start | bytes 1695752 | tf_op jit(solution)/shard_map/ppermute | solution.py:43
  245.0 13.3 %collective-permute-start.3 = (bf16[2,6,92,256]{3,2,1,0:T(8,128)(2,1)S(1)}, bf16[2,6,92,256]{3,2,1,0:T(8,128)(2,1)S(1)}, u32[]{:S(2)}, u32[]{:S(2)}) collective-permute-start(bf16[2,6,92,256]{3,2,1,0:T(8,128)(2,1)S(1)} %get-tuple-element.92), channel_id=1, source_target_pairs={{1,0},{2,1},{3,2},{4,3},{5,4},{6,5},{7,6},{8,7},{9,8},{10,9},{11,1... | collective-permute-start | bytes 1695752 | tf_op jit(solution)/shard_map/ppermute | solution.py:45
where the time goes:
time: 282 us; the launch traced here: 281 us
  other arithmetic  144 us (51%)
  waiting for transfers between devices  64.8 us (23%)
  starting transfers between devices  46.2 us (16%)
  local copies, waits for them, and re-layouts  21.1 us (7%)
  loops' own time  3.95 us (1%)
    reduce_sum x6, other arithmetic, var_density(): total = jnp.sum(jnp.exp(-0.5 * scaled * scaled), axis=0)  115 us
    all_to_all x2, waiting for transfers between devices, cut_exchange(): lax.all_to_all(slab, axis, split_axis=0, concat_axis=0, tiled=True)  49.7 us
    all_to_all x2, starting transfers between devices, cut_exchange(): lax.all_to_all(slab, axis, split_axis=0, concat_axis=0, tiled=True)  27.9 us
    ppermute x2, starting transfers between devices, extended(): lax.ppermute(tail, axis, [(i, (i + 1) % count) for i in range(ends)])  15.1 us
    dynamic_slice x18, local copies, waits for them, and re-layouts, block_density(): lax.map(lambda t: var_density(t[0], t[1], t[2]), (items, centers, widths))  13.8 us
    add x1, other arithmetic, shards(): padded[0:rows] + padded[1:rows + 1] + padded[2:rows + 2]  13.6 us
    ppermute x2, waiting for transfers between devices, extended(): lax.ppermute(head, axis, [((i + 1) % count, i) for i in range(ends)])  10.2 us
  transfers between devices with their start and end apart: 6, of which 6 were waited for; matrix products, arithmetic and copies ran while one was open for 0% of the time, Pallas kernels for 0%

commit v1 on v0

v1 whole, which is shorter than its diff:
```python
import math

import jax
import jax.numpy as jnp
from jax import lax
from jax.experimental import pallas as pl
from jax.experimental.pallas import tpu as pltpu
from jax.sharding import PartitionSpec as P

F32, BF16, I32 = jnp.float32, jnp.bfloat16, jnp.int32
SECTORS, ROWS, VARS, CELLS, BINS = 16, 12, 6, 88, 256
WIDE = 96
LEVELS = 5
FEATURES = LEVELS * 256


def packed_codes(codes, exponents):
    c = codes.astype(BF16)
    c = jnp.pad(c, ((0, 0), (0, 0), (0, 0), (2, WIDE - CELLS - 2)))
    s = jnp.stack([c[..., CELLS * j : CELLS * j + WIDE] for j in range(SECTORS)])
    s = s.reshape(SECTORS, 4, 3, 4, VARS, WIDE)
    s = jnp.transpose(s, (0, 2, 4, 1, 3, 5)).reshape(SECTORS, 3, VARS, 4, 3, 128)
    s = jnp.transpose(s, (0, 1, 4, 2, 3, 5)).reshape(SECTORS, 216, 128)
    e = jnp.pad((exponents + 8).astype(BF16).reshape(-1), (0, 8 * 128 - 288))
    e = jnp.broadcast_to(e.reshape(1, 8, 128), (SECTORS, 8, 128))
    return jnp.concatenate([s, e], axis=1)


def levels_of(rows):
    n = rows.shape[0]
    return rows.reshape(n, 8 * 128)[:, :288].astype(I32).reshape(n * 4, ROWS, VARS)


def kernel_table(centers, widths):
    f = jnp.arange(FEATURES)
    level, byte, word = f // 256, (f // 64) % 4, f % 64
    x = (4 * word + byte - 128).astype(F32) * jnp.exp2((level - 8).astype(F32))
    d = (centers[:, :, None] - x[None, None, :]) / widths[:, None, None]
    return jnp.exp(-0.5 * d * d).astype(BF16)


def density_kernel(lev, scale, flag, r_ref, fr_ref, fl_ref, t_ref, s_ref, o_ref, hi, val, acc0, acc1, a_ref, p_ref):
    step = pl.program_id(0)
    lane = lax.broadcasted_iota(I32, (SECTORS, 8, 128), 2)

    def tile(ref, k):
        start = pl.multiple_of(k * 24 + step * 8, 8)
        return ref[:, pl.ds(start, 8), :].astype(F32)

    def put(rr, x):
        c = x.astype(I32) + 128
        hi[rr] = lax.shift_right_logical(c, 2)
        val[rr] = lax.shift_left(jnp.ones_like(c), (c & 3) * 8)

    for g in range(4):
        if g < 3:
            t0, t1, t2 = (tile(r_ref, g * 3 + k) for k in range(3))
        else:
            t0, t2 = tile(fr_ref, 0), tile(fl_ref, 1)
            t1 = jnp.where(lane < 64, tile(fr_ref, 1), tile(fl_ref, 0))
        put(4 * g, t0)
        put(4 * g + 1, jnp.where(lane < 32, pltpu.roll(t0, 32, 2), pltpu.roll(t1, 32, 2)))
        put(4 * g + 2, jnp.where(lane < 64, pltpu.roll(t1, 64, 2), pltpu.roll(t2, 64, 2)))
        put(4 * g + 3, pltpu.roll(t2, 96, 2))

    words = lax.broadcasted_iota(I32, (64, 128), 0)

    @pl.loop(0, 16)
    def _(job):
        vv = job // 8
        pair = (job % 8) * 2
        accs = (acc0, acc1)
        for acc in accs:
            acc[...] = jnp.zeros_like(acc)

        @pl.loop(0, SECTORS)
        def _(src):
            for mm in range(4):
                for q in range(2):
                    e = lev[(step * 2 + vv) * 16 + pair + q, src * 4 + mm]
                    row = pl.ds(vv * 4 + mm, 1)
                    h = jnp.broadcast_to(hi[pair + q, src, row], (64, 128))
                    v = jnp.broadcast_to(val[pair + q, src, row], (64, 128))
                    pltpu.store(accs[q].at[e], accs[q][e] + v, mask=h == words)

        for q in range(2):
            for e in range(LEVELS):
                a = accs[q][e]
                for j in range(4):
                    n = lax.shift_right_logical(a, 8 * j) & 255
                    a_ref[e * 256 + j * 64 : e * 256 + j * 64 + 64, q * 128 : q * 128 + 128] = n.astype(F32).astype(BF16)
        d = jnp.dot(t_ref[vv], a_ref[...], preferred_element_type=F32).astype(BF16)
        for q in range(2):
            rr = pair + q
            p = lax.dot_general(s_ref[...], d[:, q * 128 : q * 128 + 128], (((1,), (1,)), ((), ())), preferred_element_type=F32)
            p_ref[vv, lax.rem(rr + 2, 16)] = p * flag[rr]

    for vv in range(2):

        @pl.loop(0, ROWS)
        def _(r):
            total = p_ref[vv, r]
            for k in range(1, 5):
                total = total + p_ref[vv, r + k]
            o_ref[r, vv] = (total[:CELLS] * scale[step * 2 + vv]).astype(BF16)


def densities(lev, scale, flag, owned, right, left, table, window):
    smem = pl.BlockSpec(memory_space=pltpu.SMEM)
    vmem = pl.BlockSpec(memory_space=pltpu.VMEM)
    return pl.pallas_call(
        density_kernel,
        out_shape=jax.ShapeDtypeStruct((ROWS, VARS, CELLS, BINS), BF16),
        grid=(3,),
        in_specs=[smem, smem, smem, vmem, vmem, vmem, pl.BlockSpec((2, BINS, FEATURES), lambda i: (i, 0, 0)), vmem],
        out_specs=pl.BlockSpec((ROWS, 2, CELLS, BINS), lambda i: (0, i, 0, 0)),
        scratch_shapes=[
            pltpu.VMEM((16, SECTORS, 8, 128), I32),
            pltpu.VMEM((16, SECTORS, 8, 128), I32),
            pltpu.VMEM((LEVELS, 64, 128), I32),
            pltpu.VMEM((LEVELS, 64, 128), I32),
            pltpu.VMEM((FEATURES, 256), BF16),
            pltpu.VMEM((2, 16, WIDE, BINS), F32),
        ],
        compiler_params=pltpu.CompilerParams(vmem_limit_bytes=56 << 20),
        cost_estimate=pl.CostEstimate(flops=10**10, bytes_accessed=10**7, transcendentals=0),
    )(lev, scale, flag, owned, right, left, table, window)


def shards(codes, exponents, centers, widths):
    sector, band = lax.axis_index("member"), lax.axis_index("band")
    bands = lax.axis_size("band")
    owned = lax.all_to_all(packed_codes(codes, exponents), "member", split_axis=0, concat_axis=0, tiled=True)
    table = kernel_table(centers, widths)
    head = jnp.concatenate([owned[:, 0:48], owned[:, 216:224]], axis=1)
    right = lax.ppermute(head, "band", [(i + 1, i) for i in range(bands - 1)])
    left = lax.ppermute(owned[:, 168:224], "band", [(i, i + 1) for i in range(bands - 1)])
    lev = jnp.concatenate(
        [levels_of(owned[:, 216:224]), levels_of(right[:, 48:56])[:, :2], levels_of(left[:, 48:56])[:, 10:]], axis=1
    )
    lev = jnp.transpose(lev, (2, 1, 0)).reshape(VARS * 16, 64)
    scale = 1.0 / (25.0 * 64.0 * math.sqrt(2.0 * math.pi) * widths)
    rr = jnp.arange(16)
    flag = jnp.where(rr < 12, True, jnp.where(rr < 14, band < bands - 1, band > 0)).astype(F32)
    out_l, lane = jnp.arange(WIDE)[:, None], jnp.arange(128)[None, :]
    cell = sector * CELLS + lane - 2
    inside = (lane >= out_l) & (lane <= out_l + 4) & (cell >= 0) & (cell < SECTORS * CELLS) & (out_l < CELLS)
    return densities(lev, scale, flag, owned, right, left, table, inside.astype(BF16))


def solution(mesh):
    return jax.shard_map(
        shards,
        mesh=mesh,
        in_specs=(P("member", "band", None, None), P("member", "band", None), P(), P()),
        out_specs=P("band", None, "member", None),
        check_vma=False,
    )
```

time: 282 us -> 153 us (0.54)
  other arithmetic: 144 us -> 8.99 us
  Pallas kernels: 0 us -> 71.8 us
  waiting for transfers between devices: 64.8 us -> 41.6 us
  starting transfers between devices: 46.2 us -> 25.1 us
  local copies, waits for them, and re-layouts: 21.1 us -> 4.66 us
  loops' own time: 3.95 us -> 0 us
    reduce_sum x6 -> x0, other arithmetic: 115 us -> none  [var_density(): total = jnp.sum(jnp.exp(-0.5 * scaled * scaled), axis=0)]
    pallas_call x0 -> x1, Pallas kernels: none -> 71.8 us  [densities(): pl.pallas_call(density_kernel, out_shape=jax.ShapeDtypeStruct((ROWS, VARS...]
    dynamic_slice x18 -> x0, local copies, waits for them, and re-layouts: 13.8 us -> none  [block_density(): lax.map(lambda t: var_density(t[0], t[1], t[2]), (items, centers, widths))]
    add x1, other arithmetic: 13.6 us -> 0.01 us  [shards(): out_l + 4]
    all_to_all x2 -> x1, waiting for transfers between devices: 49.7 us -> 36.1 us  [shards(): lax.all_to_all(packed_codes(codes, exponents), 'member', split_axis=0, co...]
    all_to_all x2 -> x1, starting transfers between devices: 27.9 us -> 15 us  [shards(): lax.all_to_all(packed_codes(codes, exponents), 'member', split_axis=0, co...]
    ppermute x4 -> x2, waiting for transfers between devices: 15.2 us -> 5.52 us  [the longest x1 5.51 us: shards(): right = lax.ppermute(head, 'band', [(i + 1, i) for i in range(bands - 1)])]
    ppermute x4 -> x2, starting transfers between devices: 18.3 us -> 10.1 us  [the longest x1 8.15 us: shards(): lax.ppermute(owned[:, 168:224], 'band', [(i, i + 1) for i in range(bands...]
  transfers between devices with their start and end apart: 6 -> 3, of which waited for: 6 -> 2; matrix products, arithmetic and copies ran while one was open for 0% -> 4% of each run, Pallas kernels for 0% -> 0%
where the time goes in v1:
time: 153 us; the launch traced here: 152 us
  Pallas kernels  71.8 us (47%)
  waiting for transfers between devices  41.6 us (27%)
  starting transfers between devices  25.1 us (16%)
  other arithmetic  8.99 us (6%)
  local copies, waits for them, and re-layouts  4.66 us (3%)
    pallas_call x1, Pallas kernels, densities(): pl.pallas_call(density_kernel, out_shape=jax.ShapeDtypeStruct((ROWS, VARS...  71.8 us
    all_to_all x1, waiting for transfers between devices, shards(): lax.all_to_all(packed_codes(codes, exponents), 'member', split_axis=0, co...  36.1 us
    all_to_all x1, starting transfers between devices, shards(): lax.all_to_all(packed_codes(codes, exponents), 'member', split_axis=0, co...  15 us
    ppermute x1, starting transfers between devices, shards(): lax.ppermute(owned[:, 168:224], 'band', [(i, i + 1) for i in range(bands...  8.15 us
    ppermute x1, waiting for transfers between devices, shards(): right = lax.ppermute(head, 'band', [(i + 1, i) for i in range(bands - 1)])  5.51 us
    convert_element_type x1, other arithmetic, kernel_table(): return jnp.exp(-0.5 * d * d).astype(BF16)  3.08 us
  transfers between devices with their start and end apart: 3, of which 2 were waited for; matrix products, arithmetic and copies ran while one was open for 4% of the time, Pallas kernels for 0%

profile of v1, /device:TPU:7, one launch (start us, length us, event | category | flops | bytes accessed | tf_op | source)
XLA Modules:
  0.0 152.5 jit_solution(14394841181055071743)
XLA Ops:
  0.0 0.7 add_convert_fusion
  0.7 0.1 copy.44
  0.8 0.1 reshape.144
  1.0 1.7 %convert_element_type.36 = bf16[4,12,6,1408]{3,0,2,1:T(4,128)(2,1)S(1)} convert(s32[4,12,6,1408]{3,0,2,1:T(4,128)} %param.4) | non-fusion elementwise | flops 405504 | bytes 2433024 | tf_op jit(solution)/shard_map/convert_element_type | solution.py:18
  2.7 0.7 pad_slice_fusion
  4.1 0.8 reshape.142
  4.9 0.4 copy.43
  5.3 1.0 pad_maximum_fusion
  6.2 0.0 copy-start.4
  6.2 0.0 copy-start.1
  6.3 15.0 %all-to-all-start = ((bf16[16,224,128]{2,1,0:T(8,128)(2,1)}), bf16[16,224,128]{2,1,0:T(8,128)(2,1)S(1)}, u32[]{:S(2)}, u32[]{:S(2)}) async-start(bf16[16,224,128]{2,1,0:T(8,128)(2,1)} %pad_maximum_fusion), calls=%async_computation | async-start | bytes 1835008 | tf_op jit(solution)/shard_map/all_to_all | solution.py:133
  21.4 0.0 copy-done.4
  21.4 0.6 multiply_divide_fusion.scale
  22.0 0.0 copy-done.1
  22.0 3.1 %fusion.1.t_ref = bf16[6,256,1280]{2,1,0:T(8,128)(2,1)} fusion(f32[6]{0:T(128)S(1)} %copy-done.4, f32[1280]{0:T(1024)S(1)} %fusion.17, f32[6,256]{1,0:T(8,128)S(1)} %copy-done.1), kind=kLoop, calls=%fused_computation.2 | loop fusion | flops 9830400 | bytes 3943448 | tf_op jit(solution)/shard_map/convert_element_type | solution.py:39
  25.1 36.1 %all-to-all-done.r_ref = bf16[16,224,128]{2,1,0:T(8,128)(2,1)S(1)} async-done(((bf16[16,224,128]{2,1,0:T(8,128)(2,1)}), bf16[16,224,128]{2,1,0:T(8,128)(2,1)S(1)}, u32[]{:S(2)}, u32[]{:S(2)}) %all-to-all-start) | async-done | bytes 917536 | tf_op jit(solution)/shard_map/all_to_all | solution.py:133
  61.2 0.0 copy-start
  61.2 8.1 %collective-permute-start.1 = (bf16[16,56,128]{2,1,0:T(8,128)(2,1)S(1)}, bf16[16,56,128]{2,1,0:T(8,128)(2,1)S(1)}, u32[]{:S(2)}, u32[]{:S(2)}) collective-permute-start(bf16[16,56,128]{2,1,0:T(8,128)(2,1)S(1)} %slice.141), channel_id=1, source_target_pairs={{0,1},{1,2},{2,3},{3,4},{4,5},{5,6},{6,7},{7,8},{8,9},{9,10},{10,1... | collective-permute-start | bytes 688136 | tf_op jit(solution)/shard_map/ppermute | solution.py:137
  69.4 1.9 %collective-permute-start = (bf16[16,56,128]{2,1,0:T(8,128)(2,1)S(1)}, bf16[16,56,128]{2,1,0:T(8,128)(2,1)S(1)}, u32[]{:S(2)}, u32[]{:S(2)}) collective-permute-start(bf16[16,56,128]{2,1,0:T(8,128)(2,1)S(1)} %pad_maximum_fusion.1), channel_id=1, source_target_pairs={{1,0},{2,1},{3,2},{4,3},{5,4},{6,5},{7,6},{8,7},{9,8},{10,9},{11,1... | collective-permute-start | bytes 688136 | tf_op jit(solution)/shard_map/ppermute | solution.py:136
  71.3 0.5 select_convert_fusion.flag
  71.9 0.7 fusion.6.s_ref
  72.6 0.4 reshape.146
  73.0 0.3 copy.45
  73.3 0.0 collective-permute-done.1.fl_ref
  73.3 0.0 copy-start.2
  73.4 5.5 %collective-permute-done.fr_ref = bf16[16,56,128]{2,1,0:T(8,128)(2,1)S(1)} collective-permute-done((bf16[16,56,128]{2,1,0:T(8,128)(2,1)S(1)}, bf16[16,56,128]{2,1,0:T(8,128)(2,1)S(1)}, u32[]{:S(2)}, u32[]{:S(2)}) %collective-permute-start) | collective-permute-done | bytes 229408 | tf_op jit(solution)/shard_map/ppermute | solution.py:136
  78.9 0.0 copy-start.3
  78.9 0.0 copy-done
  78.9 0.4 reshape.148
  79.4 0.1 copy.46
  79.5 0.4 reshape.150
  80.0 0.1 copy.47
  80.1 0.6 maximum_convert_fusion
  80.7 0.0 copy-done.2
  80.7 0.0 copy-done.3
  80.7 71.8 %shard_map.46 = bf16[12,6,88,256]{3,2,1,0:T(8,128)(2,1)} custom-call(s32[96,64]{1,0:T(8,128)} %bitcast.61, f32[6]{0:T(128)} %multiply_divide_fusion.scale, f32[16]{0:T(128)} %select_convert_fusion.flag, bf16[16,224,128]{2,1,0:T(8,128)(2,1)} %copy-done, bf16[16,56,128]{2,1,0:T(8,128)(2,1)} %copy-done.3, bf16[16,56,128]{2,1,0:T(8,128)(2,1)} %copy-done.2, ...), custom_call_target="tpu_custom_call" | custom-call | flops 10000000000 | bytes 10000000 | tf_op jit(solution)/shard_map/pallas_call | solution.py:111
  (36 shorter events, 0.8 us)
Async XLA Ops:
  6.2 15.1 %copy-start.4 = (f32[6]{0:T(128)S(1)}, f32[6]{0:T(128)}, u32[]{:S(2)}) copy-start(f32[6]{0:T(128)} %param.7) | copy-start | bytes 76
  6.2 15.7 %copy-start.1 = (f32[6,256]{1,0:T(8,128)S(1)}, f32[6,256]{1,0:T(8,128)}, u32[]{:S(2)}) copy-start(f32[6,256]{1,0:T(8,128)} %param.6) | copy-start | bytes 18436
  6.3 54.9 %all-to-all-start = ((bf16[16,224,128]{2,1,0:T(8,128)(2,1)}), bf16[16,224,128]{2,1,0:T(8,128)(2,1)S(1)}, u32[]{:S(2)}, u32[]{:S(2)}) async-start(bf16[16,224,128]{2,1,0:T(8,128)(2,1)} %pad_maximum_fusion), calls=%async_computation | async-start | bytes 1835008 | tf_op jit(solution)/shard_map/all_to_all | solution.py:133
  61.2 17.7 %copy-start = (bf16[16,224,128]{2,1,0:T(8,128)(2,1)}, bf16[16,224,128]{2,1,0:T(8,128)(2,1)S(1)}, u32[]{:S(2)}) copy-start(bf16[16,224,128]{2,1,0:T(8,128)(2,1)S(1)} %all-to-all-done.r_ref) | copy-start | bytes 2752516
  61.2 12.1 %collective-permute-start.1 = (bf16[16,56,128]{2,1,0:T(8,128)(2,1)S(1)}, bf16[16,56,128]{2,1,0:T(8,128)(2,1)S(1)}, u32[]{:S(2)}, u32[]{:S(2)}) collective-permute-start(bf16[16,56,128]{2,1,0:T(8,128)(2,1)S(1)} %slice.141), channel_id=1, source_target_pairs={{0,1},{1,2},{2,3},{3,4},{4,5},{5,6},{6,7},{7,8},{8,9},{9,10},{10,1... | collective-permute-start | bytes 688136 | tf_op jit(solution)/shard_map/ppermute | solution.py:137
  69.4 9.4 %collective-permute-start = (bf16[16,56,128]{2,1,0:T(8,128)(2,1)S(1)}, bf16[16,56,128]{2,1,0:T(8,128)(2,1)S(1)}, u32[]{:S(2)}, u32[]{:S(2)}) collective-permute-start(bf16[16,56,128]{2,1,0:T(8,128)(2,1)S(1)} %pad_maximum_fusion.1), channel_id=1, source_target_pairs={{1,0},{2,1},{3,2},{4,3},{5,4},{6,5},{7,6},{8,7},{9,8},{10,9},{11,1... | collective-permute-start | bytes 688136 | tf_op jit(solution)/shard_map/ppermute | solution.py:136
  73.3 7.4 %copy-start.2 = (bf16[16,56,128]{2,1,0:T(8,128)(2,1)}, bf16[16,56,128]{2,1,0:T(8,128)(2,1)S(1)}, u32[]{:S(2)}) copy-start(bf16[16,56,128]{2,1,0:T(8,128)(2,1)S(1)} %collective-permute-done.1.fl_ref) | copy-start | bytes 688132
  78.9 1.8 %copy-start.3 = (bf16[16,56,128]{2,1,0:T(8,128)(2,1)}, bf16[16,56,128]{2,1,0:T(8,128)(2,1)S(1)}, u32[]{:S(2)}) copy-start(bf16[16,56,128]{2,1,0:T(8,128)(2,1)S(1)} %collective-permute-done.fr_ref) | copy-start | bytes 688132

commit v2 on v1

v2 whole, which is shorter than its diff:
```python
import math

import jax
import jax.numpy as jnp
from jax import lax
from jax.experimental import pallas as pl
from jax.experimental.pallas import tpu as pltpu
from jax.sharding import PartitionSpec as P

F32, BF16, I32 = jnp.float32, jnp.bfloat16, jnp.int32
SECTORS, ROWS, VARS, CELLS, BINS = 16, 12, 6, 88, 256
WIDE = 96
LEVELS = 5
FEATURES = LEVELS * 256
QUAD = 4
SMEM = pl.BlockSpec(memory_space=pltpu.SMEM)
VMEM = pl.BlockSpec(memory_space=pltpu.VMEM)


def packed_codes(codes):
    groups = codes.shape[1] // 4
    c = jnp.pad(codes.astype(BF16), ((0, 0), (0, 0), (0, 0), (2, WIDE - CELLS - 2)))
    s = jnp.stack([c[..., CELLS * j : CELLS * j + WIDE] for j in range(SECTORS)])
    s = s.reshape(SECTORS, 4, groups, 4, VARS, WIDE)
    s = jnp.transpose(s, (0, 2, 4, 1, 3, 5)).reshape(SECTORS, groups, VARS, 4, 3, 128)
    return jnp.transpose(s, (0, 1, 4, 2, 3, 5)).reshape(SECTORS, groups * 72, 128)


def packed_levels(exponents):
    e = jnp.pad((exponents + 8).astype(BF16).reshape(4, ROWS * VARS), ((0, 4), (0, 128 - ROWS * VARS)))
    return jnp.broadcast_to(e[None], (SECTORS, 8, 128))


def levels_of(rows):
    return rows[:, :4, : ROWS * VARS].astype(I32).reshape(4 * SECTORS, ROWS * VARS)


def kernel_table(centers, widths):
    f = jnp.arange(FEATURES)
    level, byte, word = f // 256, (f // 64) % 4, f % 64
    x = (4 * word + byte - 128).astype(F32) * jnp.exp2((level - 8).astype(F32))
    d = (centers[:, :, None] - x[None, None, :]) / widths[:, None, None]
    return jnp.exp(-0.5 * d * d).astype(BF16)


def unpack(quad, t0, t1, t2, word, bit):
    lane = lax.broadcasted_iota(I32, (SECTORS, 8, 128), 2)

    def put(k, x):
        c = x.astype(I32) + 128
        word[quad * 4 + k] = lax.shift_right_logical(c, 2)
        bit[quad * 4 + k] = lax.shift_left(jnp.ones_like(c), (c & 3) * 8)

    put(0, t0)
    put(1, jnp.where(lane < 32, pltpu.roll(t0, 32, 2), pltpu.roll(t1, 32, 2)))
    put(2, jnp.where(lane < 64, pltpu.roll(t1, 64, 2), pltpu.roll(t2, 64, 2)))
    put(3, pltpu.roll(t2, 96, 2))


def tile_of(ref, k):
    start = pl.multiple_of(k * 24 + pl.program_id(0) * 8, 8)
    return ref[:, pl.ds(start, 8), :].astype(F32)


def row_sums(lev, t_ref, s_ref, word, bit, a_ref, accs, put):
    step = pl.program_id(0)
    words = lax.broadcasted_iota(I32, (64, 128), 0)
    for acc in accs:
        acc[...] = jnp.zeros_like(acc)

    @pl.loop(0, 4)
    def _(job):
        vv = job // 2
        first = (job % 2) * QUAD

        @pl.loop(0, SECTORS // 4)
        def _(block):
            for k in range(16):
                src, mm = block * 4 + k // 4, k % 4
                for q in range(QUAD):
                    e = lev[src * 4 + mm, (first + q) * VARS + step * 2 + vv]
                    at = pl.ds(vv * 4 + mm, 1)
                    h = jnp.broadcast_to(word[first + q, src, at], (64, 128))
                    v = jnp.broadcast_to(bit[first + q, src, at], (64, 128))
                    accs[q][e] = accs[q][e] + jnp.where(h == words, v, 0)

        for q in range(QUAD):
            for e in range(LEVELS):
                a = accs[q][e]
                accs[q][e] = jnp.zeros_like(a)
                for j in range(4):
                    n = lax.shift_right_logical(a, 8 * j) & 255
                    a_ref[e * 256 + j * 64 : e * 256 + j * 64 + 64, q * 128 : q * 128 + 128] = n.astype(F32).astype(BF16)

        d = jnp.dot(t_ref[vv], a_ref[...], preferred_element_type=F32).astype(BF16)
        for q in range(QUAD):
            p = lax.dot_general(s_ref[...], d[:, q * 128 : q * 128 + 128], (((1,), (1,)), ((), ())), preferred_element_type=F32)
            put(first + q, vv, p)


def outer_kernel(lev, r_ref, t_ref, s_ref, p_ref, word, bit, a_ref, *accs):
    for quad in range(2):
        unpack(quad, *(tile_of(r_ref, quad * 3 + k) for k in range(3)), word, bit)

    def put(k, vv, p):
        p_ref[k, vv] = p

    row_sums(lev, t_ref, s_ref, word, bit, a_ref, accs, put)


def inner_kernel(lev, scale, flag, r_ref, fr_ref, fl_ref, p_ref, t_ref, s_ref, o_ref, own, word, bit, a_ref, *accs):
    lane = lax.broadcasted_iota(I32, (SECTORS, 8, 128), 2)
    unpack(0, tile_of(fr_ref, 0), jnp.where(lane < 64, tile_of(fr_ref, 1), tile_of(fl_ref, 0)), tile_of(fl_ref, 1), word, bit)
    unpack(1, *(tile_of(r_ref, k) for k in range(3)), word, bit)

    def put(k, vv, p):
        own[k, vv] = p * flag[k]

    row_sums(lev, t_ref, s_ref, word, bit, a_ref, accs, put)
    rows = [(own, 2), (own, 3)] + [(p_ref, k) for k in range(4)] + [(own, k) for k in range(4, 8)]
    rows += [(p_ref, k) for k in range(4, 8)] + [(own, 0), (own, 1)]

    @pl.loop(0, 2)
    def _(vv):
        factor = scale[pl.program_id(0) * 2 + vv]
        for r in range(ROWS):
            ref, k = rows[r]
            total = ref[k, vv]
            for ref, k in rows[r + 1 : r + 5]:
                total = total + ref[k, vv]
            o_ref[r, vv] = (total[:CELLS] * factor).astype(BF16)


SCRATCH = [
    pltpu.VMEM((8, SECTORS, 8, 128), I32),
    pltpu.VMEM((8, SECTORS, 8, 128), I32),
    pltpu.VMEM((FEATURES, QUAD * 128), BF16),
] + [pltpu.VMEM((LEVELS, 64, 128), I32)] * QUAD
PARAMS = dict(
    compiler_params=pltpu.CompilerParams(vmem_limit_bytes=48 << 20),
    cost_estimate=pl.CostEstimate(flops=10**10, bytes_accessed=10**7, transcendentals=0),
)
TABLE = pl.BlockSpec((2, BINS, FEATURES), lambda i: (i, 0, 0))
SUMS = pl.BlockSpec((8, 2, WIDE, BINS), lambda i: (0, i, 0, 0))


def outer_rows(lev, owned, table, window):
    return pl.pallas_call(
        outer_kernel,
        out_shape=jax.ShapeDtypeStruct((8, VARS, WIDE, BINS), F32),
        grid=(3,),
        in_specs=[SMEM, VMEM, TABLE, VMEM],
        out_specs=SUMS,
        scratch_shapes=SCRATCH,
        **PARAMS,
    )(lev, owned, table, window)


def all_rows(lev, scale, flag, owned, right, left, outer, table, window):
    return pl.pallas_call(
        inner_kernel,
        out_shape=jax.ShapeDtypeStruct((ROWS, VARS, CELLS, BINS), BF16),
        grid=(3,),
        in_specs=[SMEM, SMEM, SMEM, VMEM, VMEM, VMEM, SUMS, TABLE, VMEM],
        out_specs=pl.BlockSpec((ROWS, 2, CELLS, BINS), lambda i: (0, i, 0, 0)),
        scratch_shapes=[pltpu.VMEM((8, 2, WIDE, BINS), F32)] + SCRATCH,
        **PARAMS,
    )(lev, scale, flag, owned, right, left, outer, table, window)


def exchanged(x):
    return lax.all_to_all(x, "member", split_axis=0, concat_axis=0, tiled=True)


def shards(codes, exponents, centers, widths):
    sector, band = lax.axis_index("member"), lax.axis_index("band")
    bands = lax.axis_size("band")
    edges = jnp.concatenate([codes[:, :4], codes[:, 8:]], axis=1)
    first = exchanged(jnp.concatenate([packed_codes(edges), packed_levels(exponents)], axis=1))
    second = exchanged(packed_codes(codes[:, 4:8]))
    table = kernel_table(centers, widths)
    head = jnp.concatenate([first[:, :48], first[:, 144:]], axis=1)
    right = lax.ppermute(head, "band", [(i + 1, i) for i in range(bands - 1)])
    left = lax.ppermute(first[:, 96:], "band", [(i, i + 1) for i in range(bands - 1)])
    lev = levels_of(first[:, 144:])
    outer_lev = jnp.concatenate([lev[:, :24], lev[:, 48:]], axis=1)
    inner_lev = jnp.concatenate([levels_of(right[:, 48:])[:, :12], levels_of(left[:, 48:])[:, 60:], lev[:, 24:48]], axis=1)
    scale = 1.0 / (25.0 * 64.0 * math.sqrt(2.0 * math.pi) * widths)
    k = jnp.arange(8)
    flag = jnp.where(k >= 4, True, jnp.where(k < 2, band < bands - 1, band > 0)).astype(F32)
    out_l, lane = jnp.arange(WIDE)[:, None], jnp.arange(128)[None, :]
    cell = sector * CELLS + lane - 2
    window = (lane >= out_l) & (lane <= out_l + 4) & (cell >= 0) & (cell < SECTORS * CELLS) & (out_l < CELLS)
    window = window.astype(BF16)
    outer = outer_rows(outer_lev, first, table, window)
    return all_rows(inner_lev, scale, flag, second, right, left, outer, table, window)


def solution(mesh):
    return jax.shard_map(
        shards,
        mesh=mesh,
        in_specs=(P("member", "band", None, None), P("member", "band", None), P(), P()),
        out_specs=P("band", None, "member", None),
        check_vma=False,
    )
```

time: 153 us -> 122 us (0.80)
  the two profiles are of different devices: /device:TPU:7 before, /device:TPU:48 now
where the time goes in v2:
time: 122 us; the launch traced here: 121 us
  Pallas kernels  48.5 us (40%)
  starting transfers between devices  29.9 us (25%)
  waiting for transfers between devices  26.4 us (22%)
  local copies, waits for them, and re-layouts  8.99 us (7%)
  other arithmetic  7.22 us (6%)
    all_to_all x2, waiting for transfers between devices, exchanged(): return lax.all_to_all(x, 'member', split_axis=0, concat_axis=0, tiled=True)  26.4 us
    pallas_call x1, Pallas kernels, all_rows(): pl.pallas_call(inner_kernel, out_shape=jax.ShapeDtypeStruct((ROWS, VARS,...  24.9 us
    pallas_call x1, Pallas kernels, outer_rows(): pl.pallas_call(outer_kernel, out_shape=jax.ShapeDtypeStruct((8, VARS, WID...  23.6 us
    all_to_all x2, starting transfers between devices, exchanged(): return lax.all_to_all(x, 'member', split_axis=0, concat_axis=0, tiled=True)  22.2 us
    unnamed x40, local copies, waits for them, and re-layouts  6.06 us
    ppermute x1, starting transfers between devices, shards(): right = lax.ppermute(head, 'band', [(i + 1, i) for i in range(bands - 1)])  5.75 us
    convert_element_type x1, other arithmetic, kernel_table(): return jnp.exp(-0.5 * d * d).astype(BF16)  3.19 us
  transfers between devices with their start and end apart: 4, of which 1 were waited for; matrix products, arithmetic and copies ran while one was open for 5% of the time, Pallas kernels for 19%

profile of v2, /device:TPU:48, one launch (start us, length us, event | category | flops | bytes accessed | tf_op | source)
XLA Modules:
  0.0 121.4 jit_solution(16631775561261221346)
XLA Ops:
  0.0 1.7 %convert.12 = bf16[4,12,6,1408]{3,0,2,1:T(4,128)(2,1)S(1)} convert(s32[4,12,6,1408]{3,0,2,1:T(4,128)} %param.4) | non-fusion elementwise | flops 405504 | bytes 2433024 | tf_op jit(solution)/shard_map/convert.9
  1.7 0.3 fusion.44
  2.0 0.2 fusion.14
  2.3 0.4 fusion.15
  2.7 0.4 pad_maximum_fusion
  3.1 0.1 copy.22
  3.2 0.1 reshape.140
  3.3 0.1 pad_slice_fusion.28
  3.8 0.0 copy-start.4
  3.9 0.0 copy-start.3
  4.0 0.5 reshape.138
  4.5 0.3 copy.21
  4.8 0.9 pad_maximum_fusion.1
  5.7 15.2 %all-to-all-start = ((bf16[16,152,128]{2,1,0:T(8,128)(2,1)}), bf16[16,152,128]{2,1,0:T(8,128)(2,1)S(1)}, u32[]{:S(2)}, u32[]{:S(2)}) async-start(bf16[16,152,128]{2,1,0:T(8,128)(2,1)} %pad_maximum_fusion.1), calls=%async_computation | async-start | bytes 1245184 | tf_op jit(solution)/shard_map/all_to_all | solution.py:172
  20.9 0.1 constant_dynamic-update-slice_fusion.31
  21.0 0.1 constant_dynamic-update-slice_fusion.30
  21.1 0.1 constant_dynamic-update-slice_fusion.29
  21.2 0.1 constant_dynamic-update-slice_fusion.28
  21.3 0.1 constant_dynamic-update-slice_fusion.27
  21.4 0.1 constant_dynamic-update-slice_fusion.26
  21.5 0.1 constant_dynamic-update-slice_fusion.25
  21.6 0.1 constant_dynamic-update-slice_fusion.24
  21.7 0.1 constant_dynamic-update-slice_fusion.23
  21.8 0.1 constant_dynamic-update-slice_fusion.22
  21.9 0.1 constant_dynamic-update-slice_fusion.21
  22.0 0.1 constant_dynamic-update-slice_fusion.20
  22.1 0.1 constant_dynamic-update-slice_fusion.19
  22.1 0.1 constant_dynamic-update-slice_fusion.18
  22.2 0.1 constant_dynamic-update-slice_fusion.17
  22.3 0.1 constant_dynamic-update-slice_fusion.16
  22.5 0.2 copy.23
  22.6 0.2 reshape.146
  22.9 0.9 copy.24
  23.8 0.1 fusion.20.s_ref
  23.9 3.2 %fusion.1.t_ref = bf16[6,256,1280]{2,1,0:T(8,128)(2,1)} fusion(f32[6]{0:T(128)S(1)} %copy-done.4, f32[1280]{0:T(1024)S(1)} %fusion.33, f32[6,256]{1,0:T(8,128)S(1)} %copy-done.3), kind=kLoop, calls=%fused_computation.2 | loop fusion | flops 9830400 | bytes 3943448 | tf_op jit(solution)/shard_map/convert_element_type | solution.py:43
  27.1 26.4 %all-to-all-done.r_ref = bf16[16,152,128]{2,1,0:T(8,128)(2,1)S(1)} async-done(((bf16[16,152,128]{2,1,0:T(8,128)(2,1)}), bf16[16,152,128]{2,1,0:T(8,128)(2,1)S(1)}, u32[]{:S(2)}, u32[]{:S(2)}) %all-to-all-start) | async-done | bytes 622624 | tf_op jit(solution)/shard_map/all_to_all | solution.py:172
  53.4 7.0 %all-to-all-start.1 = ((bf16[16,72,128]{2,1,0:T(8,128)(2,1)}), bf16[16,72,128]{2,1,0:T(8,128)(2,1)S(1)}, u32[]{:S(2)}, u32[]{:S(2)}) async-start(bf16[16,72,128]{2,1,0:T(8,128)(2,1)} %bitcast.41), calls=%async_computation.1 | async-start | bytes 589824 | tf_op jit(solution)/shard_map/all_to_all | solution.py:172
  60.5 0.1 fusion.45
  60.6 1.9 %collective-permute-start.1 = (bf16[16,56,128]{2,1,0:T(8,128)(2,1)S(1)}, bf16[16,56,128]{2,1,0:T(8,128)(2,1)S(1)}, u32[]{:S(2)}, u32[]{:S(2)}) collective-permute-start(bf16[16,56,128]{2,1,0:T(8,128)(2,1)S(1)} %slice.277), channel_id=1, source_target_pairs={{0,1},{1,2},{2,3},{3,4},{4,5},{5,6},{6,7},{7,8},{8,9},{9,10},{10,1... | collective-permute-start | bytes 688136 | tf_op jit(solution)/shard_map/ppermute | solution.py:184
  62.6 5.8 %collective-permute-start = (bf16[16,56,128]{2,1,0:T(8,128)(2,1)S(1)}, bf16[16,56,128]{2,1,0:T(8,128)(2,1)S(1)}, u32[]{:S(2)}, u32[]{:S(2)}) collective-permute-start(bf16[16,56,128]{2,1,0:T(8,128)(2,1)S(1)} %pad_maximum_fusion.2), channel_id=1, source_target_pairs={{1,0},{2,1},{3,2},{4,3},{5,4},{6,5},{7,6},{8,7},{9,8},{10,9},{11,1... | collective-permute-start | bytes 688136 | tf_op jit(solution)/shard_map/ppermute | solution.py:183
  68.4 0.1 pad_add_fusion.1.lev
  68.5 2.1 %copy-done = bf16[6,256,1280]{2,1,0:T(8,128)(2,1)S(1)} copy-done((bf16[6,256,1280]{2,1,0:T(8,128)(2,1)S(1)}, bf16[6,256,1280]{2,1,0:T(8,128)(2,1)}, u32[]{:S(2)}) %copy-start) | copy-done | bytes 3932184
  70.6 23.6 %shard_map.46.p_ref = f32[8,6,96,256]{3,2,1,0:T(8,128)} custom-call(s32[64,48]{1,0:T(8,128)S(1)} %pad_add_fusion.1.lev, bf16[16,152,128]{2,1,0:T(8,128)(2,1)S(1)} %all-to-all-done.r_ref, bf16[6,256,1280]{2,1,0:T(8,128)(2,1)S(1)} %copy-done, bf16[96,128]{1,0:T(8,128)(2,1)S(1)} %fusion.20.s_ref), custom_call_target="tpu_custom_call" | custom-call | flops 10000000000 | bytes 10000000 | tf_op jit(solution)/shard_map/pallas_call | solution.py:148
  94.2 0.0 collective-permute-done.fr_ref
  94.2 0.1 slice_convert_fusion
  94.3 0.1 pad_add_fusion.lev
  94.4 2.1 %copy-done.1 = bf16[6,256,1280]{2,1,0:T(8,128)(2,1)S(1)} copy-done((bf16[6,256,1280]{2,1,0:T(8,128)(2,1)S(1)}, bf16[6,256,1280]{2,1,0:T(8,128)(2,1)}, u32[]{:S(2)}) %copy-start.1) | copy-done | bytes 3932184
  96.5 24.9 %shard_map.47 = bf16[12,6,88,256]{3,2,1,0:T(8,128)(2,1)} custom-call(s32[64,48]{1,0:T(8,128)S(1)} %pad_add_fusion.lev, f32[6]{0:T(128)S(1)} %multiply_divide_fusion.scale, f32[8]{0:T(128)S(1)} %select_convert_fusion.flag, bf16[16,72,128]{2,1,0:T(8,128)(2,1)S(1)} %all-to-all-done.1.r_ref, bf16[16,56,128]{2,1,0:T(8,128)(2,1)S(1)} %collective-permute-done.fr_ref, ...), custom_call_target="tpu_custom_call" | custom-call | flops 10000000000 | bytes 10000000 | tf_op jit(solution)/shard_map/pallas_call | solution.py:160
  (42 shorter events, 0.6 us)
Async XLA Ops:
  0.0 3.1 %copy-start.2 = (s32[4,12,6]{1,0,2:T(4,128)S(1)}, s32[4,12,6]{1,0,2:T(4,128)}, u32[]{:S(2)}) copy-start(s32[4,12,6]{1,0,2:T(4,128)} %param.5) | copy-start | bytes 3460
  3.8 19.9 %copy-start.4 = (f32[6]{0:T(128)S(1)}, f32[6]{0:T(128)}, u32[]{:S(2)}) copy-start(f32[6]{0:T(128)} %param.7) | copy-start | bytes 76
  3.9 20.0 %copy-start.3 = (f32[6,256]{1,0:T(8,128)S(1)}, f32[6,256]{1,0:T(8,128)}, u32[]{:S(2)}) copy-start(f32[6,256]{1,0:T(8,128)} %param.6) | copy-start | bytes 18436
  5.7 47.8 %all-to-all-start = ((bf16[16,152,128]{2,1,0:T(8,128)(2,1)}), bf16[16,152,128]{2,1,0:T(8,128)(2,1)S(1)}, u32[]{:S(2)}, u32[]{:S(2)}) async-start(bf16[16,152,128]{2,1,0:T(8,128)(2,1)} %pad_maximum_fusion.1), calls=%async_computation | async-start | bytes 1245184 | tf_op jit(solution)/shard_map/all_to_all | solution.py:172
  53.4 40.9 %all-to-all-start.1 = ((bf16[16,72,128]{2,1,0:T(8,128)(2,1)}), bf16[16,72,128]{2,1,0:T(8,128)(2,1)S(1)}, u32[]{:S(2)}, u32[]{:S(2)}) async-start(bf16[16,72,128]{2,1,0:T(8,128)(2,1)} %bitcast.41), calls=%async_computation.1 | async-start | bytes 589824 | tf_op jit(solution)/shard_map/all_to_all | solution.py:172
  60.6 33.5 %collective-permute-start.1 = (bf16[16,56,128]{2,1,0:T(8,128)(2,1)S(1)}, bf16[16,56,128]{2,1,0:T(8,128)(2,1)S(1)}, u32[]{:S(2)}, u32[]{:S(2)}) collective-permute-start(bf16[16,56,128]{2,1,0:T(8,128)(2,1)S(1)} %slice.277), channel_id=1, source_target_pairs={{0,1},{1,2},{2,3},{3,4},{4,5},{5,6},{6,7},{7,8},{8,9},{9,10},{10,1... | collective-permute-start | bytes 688136 | tf_op jit(solution)/shard_map/ppermute | solution.py:184
  62.6 31.5 %collective-permute-start = (bf16[16,56,128]{2,1,0:T(8,128)(2,1)S(1)}, bf16[16,56,128]{2,1,0:T(8,128)(2,1)S(1)}, u32[]{:S(2)}, u32[]{:S(2)}) collective-permute-start(bf16[16,56,128]{2,1,0:T(8,128)(2,1)S(1)} %pad_maximum_fusion.2), channel_id=1, source_target_pairs={{1,0},{2,1},{3,2},{4,3},{5,4},{6,5},{7,6},{8,7},{9,8},{10,9},{11,1... | collective-permute-start | bytes 688136 | tf_op jit(solution)/shard_map/ppermute | solution.py:183
  68.5 2.1 %copy-start = (bf16[6,256,1280]{2,1,0:T(8,128)(2,1)S(1)}, bf16[6,256,1280]{2,1,0:T(8,128)(2,1)}, u32[]{:S(2)}) copy-start(bf16[6,256,1280]{2,1,0:T(8,128)(2,1)} %fusion.1.t_ref) | copy-start | bytes 11796484
  94.4 2.1 %copy-start.1 = (bf16[6,256,1280]{2,1,0:T(8,128)(2,1)S(1)}, bf16[6,256,1280]{2,1,0:T(8,128)(2,1)}, u32[]{:S(2)}) copy-start(bf16[6,256,1280]{2,1,0:T(8,128)(2,1)} %fusion.1.t_ref) | copy-start | bytes 11796484

commit v3 on v2

v3 whole, which is shorter than its diff:
```python
import math

import jax
import jax.numpy as jnp
from jax import lax
from jax.experimental import pallas as pl
from jax.experimental.pallas import tpu as pltpu
from jax.sharding import PartitionSpec as P

F32, BF16, I32 = jnp.float32, jnp.bfloat16, jnp.int32
SECTORS, ROWS, VARS, CELLS, BINS = 16, 12, 6, 88, 256
WIDE = 96
LEVELS = 5
FEATURES = LEVELS * 256
GROUPS = 1
SPLIT = 6
JOINED = 4
SMEM = pl.BlockSpec(memory_space=pltpu.SMEM)
VMEM = pl.BlockSpec(memory_space=pltpu.VMEM)


def packed_codes(codes):
    groups = codes.shape[1] // 4
    c = jnp.pad(codes.astype(BF16), ((0, 0), (0, 0), (0, 0), (2, WIDE - CELLS - 2)))
    s = jnp.stack([c[..., CELLS * j : CELLS * j + WIDE] for j in range(SECTORS)])
    s = s.reshape(SECTORS, 4, groups, 4, VARS, WIDE)
    s = jnp.transpose(s, (0, 2, 4, 1, 3, 5)).reshape(SECTORS, groups, VARS, 4, 3, 128)
    return jnp.transpose(s, (0, 1, 4, 2, 3, 5)).reshape(SECTORS, groups * 72, 128)


def packed_levels(exponents):
    e = jnp.pad((exponents + 8).astype(BF16).reshape(4, ROWS * VARS), ((0, 4), (0, 128 - ROWS * VARS)))
    return jnp.broadcast_to(e[None], (SECTORS, 8, 128))


def levels_of(rows):
    return rows[:, :4, : ROWS * VARS].astype(I32).reshape(4 * SECTORS, ROWS * VARS)


def kernel_table(centers, widths):
    f = jnp.arange(FEATURES)
    level, byte, word = f // 256, (f // 64) % 4, f % 64
    x = (4 * word + byte - 128).astype(F32) * jnp.exp2((level - 8).astype(F32))
    d = (centers[:, :, None] - x[None, None, :]) / widths[:, None, None]
    return jnp.exp(-0.5 * d * d).astype(BF16)


def unpack(quad, t0, t1, t2, word, bit):
    lane = lax.broadcasted_iota(I32, (SECTORS, 8, 128), 2)

    def put(k, x):
        c = x.astype(I32) + 128
        word[quad * 4 + k] = lax.shift_right_logical(c, 2)
        bit[quad * 4 + k, 0] = lax.shift_left(jnp.ones_like(c), (c & 3) * 8)

    put(0, t0)
    put(1, jnp.where(lane < 32, pltpu.roll(t0, 32, 2), pltpu.roll(t1, 32, 2)))
    put(2, jnp.where(lane < 64, pltpu.roll(t1, 64, 2), pltpu.roll(t2, 64, 2)))
    put(3, pltpu.roll(t2, 96, 2))


def tile_of(ref, k):
    start = pl.multiple_of(k * 24 + pl.program_id(0) * 8, 8)
    return ref[:, pl.ds(start, 8), :].astype(F32)


def row_sums(chains, lev, t_ref, s_ref, word, bit, a_ref, accs, put):
    step = pl.program_id(0)
    part = 64 // GROUPS
    words = lax.broadcasted_iota(I32, (part, 128), 0)

    @pl.loop(0, SECTORS)
    def _(src):
        for mm in range(4):
            for acc, (slot, vv) in zip(accs, chains):
                e = lev[src * 4 + mm, slot * VARS + step * 2 + vv]
                at = pl.ds(vv * 4 + mm, 1)
                here = jnp.broadcast_to(word[slot, src, at], (part, 128)) == words
                for g in range(GROUPS):
                    v = jnp.broadcast_to(bit[slot, g, src, at], (part, 128))
                    span = pl.ds(g * part, part)
                    acc[e, span] = acc[e, span] + jnp.where(here, v, 0)

    for k in range(0, 8, JOINED):
        for c in range(k, k + JOINED):
            for e in range(LEVELS):
                a = accs[c][e]
                accs[c][e] = jnp.zeros_like(a)
                for j in range(4):
                    n = lax.shift_right_logical(a, 8 * j) & 255
                    a_ref[c, e * 256 + j * 64 : e * 256 + j * 64 + 64] = n.astype(F32).astype(BF16)
        counts = jnp.concatenate([a_ref[c] for c in range(k, k + JOINED)], axis=1)
        d = jnp.dot(t_ref[chains[k][1]], counts, preferred_element_type=F32).astype(BF16)
        for i in range(JOINED):
            p = lax.dot_general(s_ref[...], d[:, i * 128 : i * 128 + 128], (((1,), (1,)), ((), ())), preferred_element_type=F32)
            put(*chains[k + i], p)


def outer_kernel(lev, r_ref, t_ref, s_ref, p_ref, part_ref, head_ref, tail_ref, word, bit, a_ref, *accs):
    for quad in range(2):
        unpack(quad, *(tile_of(r_ref, quad * 3 + k) for k in range(3)), word, bit)
    for acc in accs:
        acc[...] = jnp.zeros_like(acc)

    def put(k, vv, p):
        p_ref[k, vv] = p

    @pl.loop(0, 2)
    def _(vv):
        row_sums([(k, vv) for k in range(8)], lev, t_ref, s_ref, word, bit, a_ref, accs, put)
        for k in range(2):
            head_ref[k, vv] = p_ref[k, vv, :CELLS].astype(BF16)
            tail_ref[k, vv] = p_ref[6 + k, vv, :CELLS].astype(BF16)
        low = p_ref[0, vv, :CELLS] + p_ref[1, vv, :CELLS] + p_ref[2, vv, :CELLS]
        part_ref[0, vv] = low
        part_ref[1, vv] = low + p_ref[3, vv, :CELLS]
        high = p_ref[5, vv, :CELLS] + p_ref[6, vv, :CELLS] + p_ref[7, vv, :CELLS]
        part_ref[2, vv] = high + p_ref[4, vv, :CELLS]
        part_ref[3, vv] = high


def inner_kernel(lev, scale, r_ref, p_ref, t_ref, s_ref, o_ref, own, word, bit, a_ref, *accs):
    unpack(0, *(tile_of(r_ref, k) for k in range(3)), word, bit)
    for acc in accs:
        acc[...] = jnp.zeros_like(acc)

    def put(k, vv, p):
        own[k, vv] = p

    row_sums([(k, vv) for vv in range(2) for k in range(4)], lev, t_ref, s_ref, word, bit, a_ref, accs, put)
    rows = [(p_ref, k) for k in range(4)] + [(own, k) for k in range(4)] + [(p_ref, k) for k in range(4, 8)]

    @pl.loop(0, 2)
    def _(vv):
        factor = scale[pl.program_id(0) * 2 + vv]
        for r in range(8):
            ref, k = rows[r]
            total = ref[k, vv]
            for ref, k in rows[r + 1 : r + 5]:
                total = total + ref[k, vv]
            o_ref[r + 2, vv] = (total[:CELLS] * factor).astype(BF16)


def edge_kernel(scale, part_ref, right_ref, left_ref, done_ref, o_ref):
    end, step = pl.program_id(1), pl.program_id(0)
    for vv in range(2):
        factor = scale[step * 2 + vv]

        @pl.when(end == 0)
        def _():
            last = left_ref[1, vv].astype(F32)
            o_ref[0, vv] = ((part_ref[0, vv] + left_ref[0, vv].astype(F32) + last) * factor).astype(BF16)
            o_ref[1, vv] = ((part_ref[1, vv] + last) * factor).astype(BF16)

        @pl.when(end == 1)
        def _():
            next_ = right_ref[0, vv].astype(F32)
            o_ref[0, vv] = ((part_ref[0, vv] + next_) * factor).astype(BF16)
            o_ref[1, vv] = ((part_ref[1, vv] + next_ + right_ref[1, vv].astype(F32)) * factor).astype(BF16)


def scratch(slots):
    return [
        pltpu.VMEM((slots, SECTORS, 8, 128), I32),
        pltpu.VMEM((slots, GROUPS, SECTORS, 8, 128), I32),
        pltpu.VMEM((8, FEATURES, 128), BF16),
    ] + [pltpu.VMEM((LEVELS, 64, 128), I32)] * 8


PARAMS = dict(compiler_params=pltpu.CompilerParams(vmem_limit_bytes=52 << 20))
COST = pl.CostEstimate(flops=10**10, bytes_accessed=10**7, transcendentals=0)
TABLE = pl.BlockSpec((2, BINS, FEATURES), lambda i: (i, 0, 0))


def blocks(rows, cells=CELLS):
    return pl.BlockSpec((rows, 2, cells, BINS), lambda i: (0, i, 0, 0))


def outer_rows(lev, owned, table, window):
    shape = lambda rows, cells, dtype: jax.ShapeDtypeStruct((rows, VARS, cells, BINS), dtype)
    return pl.pallas_call(
        outer_kernel,
        out_shape=[shape(8, WIDE, F32), shape(4, CELLS, F32), shape(2, CELLS, BF16), shape(2, CELLS, BF16)],
        grid=(3,),
        in_specs=[SMEM, VMEM, TABLE, VMEM],
        out_specs=[blocks(8, WIDE), blocks(4), blocks(2), blocks(2)],
        scratch_shapes=scratch(8),
        cost_estimate=COST,
        **PARAMS,
    )(lev, owned, table, window)


def inner_rows(lev, scale, owned, outer, table, window):
    return pl.pallas_call(
        inner_kernel,
        out_shape=jax.ShapeDtypeStruct((ROWS, VARS, CELLS, BINS), BF16),
        grid=(3,),
        in_specs=[SMEM, SMEM, VMEM, blocks(8, WIDE), TABLE, VMEM],
        out_specs=blocks(ROWS),
        scratch_shapes=[pltpu.VMEM((4, 2, WIDE, BINS), F32)] + scratch(4),
        cost_estimate=COST,
        **PARAMS,
    )(lev, scale, owned, outer, table, window)


def edge_rows(scale, part, right, left, done):
    def block(where):
        return pl.BlockSpec((2, 2, CELLS, BINS), where)

    return pl.pallas_call(
        edge_kernel,
        out_shape=jax.ShapeDtypeStruct((ROWS, VARS, CELLS, BINS), BF16),
        grid=(3, 2),
        in_specs=[
            SMEM,
            block(lambda i, end: (end, i, 0, 0)),
            block(lambda i, end: (0, i, 0, 0)),
            block(lambda i, end: (0, i, 0, 0)),
            pl.BlockSpec(memory_space=pl.ANY),
        ],
        out_specs=block(lambda i, end: (end * 5, i, 0, 0)),
        input_output_aliases={4: 0},
        cost_estimate=pl.CostEstimate(flops=10**6, bytes_accessed=10**6, transcendentals=0),
        **PARAMS,
    )(scale, part, right, left, done)


def exchanged(x):
    return lax.all_to_all(x, "member", split_axis=0, concat_axis=0, tiled=True)


def shards(codes, exponents, centers, widths):
    sector = lax.axis_index("member")
    bands = lax.axis_size("band")
    edges = jnp.concatenate([codes[:, :4], codes[:, 8:]], axis=1)
    first = exchanged(jnp.concatenate([packed_codes(edges), packed_levels(exponents)], axis=1))
    second = exchanged(packed_codes(codes[:, 4:8]))
    table = kernel_table(centers, widths)
    lev = levels_of(first[:, 144:])
    outer_lev = jnp.concatenate([lev[:, :24], lev[:, 48:]], axis=1)
    scale = 1.0 / (25.0 * 64.0 * math.sqrt(2.0 * math.pi) * widths)
    out_l, lane = jnp.arange(WIDE)[:, None], jnp.arange(128)[None, :]
    cell = sector * CELLS + lane - 2
    window = (lane >= out_l) & (lane <= out_l + 4) & (cell >= 0) & (cell < SECTORS * CELLS) & (out_l < CELLS)
    window = window.astype(BF16)
    outer, part, head, tail = outer_rows(outer_lev, first, table, window)
    right = lax.ppermute(head, "band", [(i + 1, i) for i in range(bands - 1)])
    left = lax.ppermute(tail, "band", [(i, i + 1) for i in range(bands - 1)])
    done = inner_rows(lev[:, 24:48], scale, second, outer, table, window)
    return edge_rows(scale, part, right, left, done)


def solution(mesh):
    return jax.shard_map(
        shards,
        mesh=mesh,
        in_specs=(P("member", "band", None, None), P("member", "band", None), P(), P()),
        out_specs=P("band", None, "member", None),
        check_vma=False,
    )
```

time: 122 us -> 111 us (0.910)
  the two profiles are of different devices: /device:TPU:48 before, /device:TPU:7 now
where the time goes in v3:
time: 111 us; the launch traced here: 110 us
  Pallas kernels  42.1 us (38%)
  starting transfers between devices  35.9 us (32%)
  waiting for transfers between devices  20.2 us (18%)
  other arithmetic  7.03 us (6%)
  local copies, waits for them, and re-layouts  4.69 us (4%)
    all_to_all x2, starting transfers between devices, exchanged(): return lax.all_to_all(x, 'member', split_axis=0, concat_axis=0, tiled=True)  28.2 us
    pallas_call x1, Pallas kernels, outer_rows(): pl.pallas_call(outer_kernel, out_shape=[shape(8, WIDE, F32), shape(4, CEL...  23.5 us
    all_to_all x2, waiting for transfers between devices, exchanged(): return lax.all_to_all(x, 'member', split_axis=0, concat_axis=0, tiled=True)  20.2 us
    pallas_call x1, Pallas kernels, inner_rows(): pl.pallas_call(inner_kernel, out_shape=jax.ShapeDtypeStruct((ROWS, VARS,...  13.9 us
    ppermute x1, starting transfers between devices, shards(): left = lax.ppermute(tail, 'band', [(i, i + 1) for i in range(bands - 1)])  4.92 us
    pallas_call x1, Pallas kernels, edge_rows(): pl.pallas_call(edge_kernel, out_shape=jax.ShapeDtypeStruct((ROWS, VARS, C...  4.74 us
    convert_element_type x1, other arithmetic, kernel_table(): return jnp.exp(-0.5 * d * d).astype(BF16)  3.19 us
    ppermute x1, starting transfers between devices, shards(): right = lax.ppermute(head, 'band', [(i + 1, i) for i in range(bands - 1)])  2.74 us
  transfers between devices with their start and end apart: 4, of which 1 were waited for; matrix products, arithmetic and copies ran while one was open for 6% of the time, Pallas kernels for 34%

profile of v3, /device:TPU:7, one launch (start us, length us, event | category | flops | bytes accessed | tf_op | source)
XLA Modules:
  0.0 110.3 jit_solution(10905741966013575399)
XLA Ops:
  0.0 1.7 %convert.8 = bf16[4,12,6,1408]{3,0,2,1:T(4,128)(2,1)S(1)} convert(s32[4,12,6,1408]{3,0,2,1:T(4,128)} %param.4) | non-fusion elementwise | flops 405504 | bytes 2433024 | tf_op jit(solution)/shard_map/convert.5
  1.7 0.3 fusion.44
  2.0 0.4 pad_maximum_fusion
  2.4 0.4 fusion.15
  2.8 0.2 fusion.14
  3.1 0.1 copy.23
  3.2 0.1 reshape.132
  3.3 0.1 pad_slice_fusion.28
  3.8 0.0 copy-start.2
  3.9 0.0 copy-start.1
  4.0 0.5 reshape.130
  4.5 0.3 copy.22
  4.8 0.9 pad_maximum_fusion.1
  5.7 14.9 %all-to-all-start = ((bf16[16,152,128]{2,1,0:T(8,128)(2,1)}), bf16[16,152,128]{2,1,0:T(8,128)(2,1)S(1)}, u32[]{:S(2)}, u32[]{:S(2)}) async-start(bf16[16,152,128]{2,1,0:T(8,128)(2,1)} %pad_maximum_fusion.1), calls=%async_computation | async-start | bytes 1245184 | tf_op jit(solution)/shard_map/all_to_all | solution.py:229
  20.6 0.1 constant_dynamic-update-slice_fusion.31
  20.7 0.1 constant_dynamic-update-slice_fusion.30
  20.8 0.1 constant_dynamic-update-slice_fusion.29
  20.9 0.1 constant_dynamic-update-slice_fusion.28
  21.0 0.1 constant_dynamic-update-slice_fusion.27
  21.1 0.1 constant_dynamic-update-slice_fusion.26
  21.2 0.1 constant_dynamic-update-slice_fusion.25
  21.3 0.1 constant_dynamic-update-slice_fusion.24
  21.4 0.1 constant_dynamic-update-slice_fusion.23
  21.5 0.1 constant_dynamic-update-slice_fusion.22
  21.6 0.1 constant_dynamic-update-slice_fusion.21
  21.7 0.1 constant_dynamic-update-slice_fusion.20
  21.8 0.1 constant_dynamic-update-slice_fusion.19
  21.9 0.1 constant_dynamic-update-slice_fusion.18
  22.0 0.1 constant_dynamic-update-slice_fusion.17
  22.1 0.1 constant_dynamic-update-slice_fusion.16
  22.2 0.2 copy.24
  22.3 0.2 reshape.136
  22.6 0.8 copy.25
  23.5 0.0 copy-done.2
  23.5 0.1 fusion.20.s_ref
  23.6 3.2 %fusion.1.t_ref = bf16[6,256,1280]{2,1,0:T(8,128)(2,1)} fusion(f32[6]{0:T(128)S(1)} %copy-done.2, f32[1280]{0:T(1024)S(1)} %fusion.33, f32[6,256]{1,0:T(8,128)S(1)} %copy-done.1), kind=kLoop, calls=%fused_computation.2 | loop fusion | flops 9830400 | bytes 3943448 | tf_op jit(solution)/shard_map/convert_element_type | solution.py:45
  26.8 20.2 %all-to-all-done.r_ref = bf16[16,152,128]{2,1,0:T(8,128)(2,1)S(1)} async-done(((bf16[16,152,128]{2,1,0:T(8,128)(2,1)}), bf16[16,152,128]{2,1,0:T(8,128)(2,1)S(1)}, u32[]{:S(2)}, u32[]{:S(2)}) %all-to-all-start) | async-done | bytes 622624 | tf_op jit(solution)/shard_map/all_to_all | solution.py:229
  47.0 13.3 %all-to-all-start.1 = ((bf16[16,72,128]{2,1,0:T(8,128)(2,1)}), bf16[16,72,128]{2,1,0:T(8,128)(2,1)S(1)}, u32[]{:S(2)}, u32[]{:S(2)}) async-start(bf16[16,72,128]{2,1,0:T(8,128)(2,1)} %bitcast.40), calls=%async_computation.1 | async-start | bytes 589824 | tf_op jit(solution)/shard_map/all_to_all | solution.py:229
  60.3 0.1 fusion.45
  60.4 0.1 pad_add_fusion.lev
  60.5 23.5 %shard_map.46 = (f32[8,6,96,256]{3,2,1,0:T(8,128)}, f32[4,6,88,256]{3,2,1,0:T(8,128)}, bf16[2,6,88,256]{3,2,1,0:T(8,128)(2,1)S(1)}, bf16[2,6,88,256]{3,2,1,0:T(8,128)(2,1)S(1)}) custom-call(s32[64,48]{1,0:T(8,128)S(1)} %pad_add_fusion.lev, bf16[16,152,128]{2,1,0:T(8,128)(2,1)S(1)} %all-to-all-done.r_ref, bf16[6,256,1280]{2,1,0:T(8,128)(2,1)} %fusion.1.t_ref, ...), custom_call_target="tpu_custom_call" | custom-call | flops 10000000000 | bytes 10000000 | tf_op jit(solution)/shard_map/pallas_call | solution.py:181
  84.0 2.7 %collective-permute-start = (bf16[2,6,88,256]{3,2,1,0:T(8,128)(2,1)S(1)}, bf16[2,6,88,256]{3,2,1,0:T(8,128)(2,1)S(1)}, u32[]{:S(2)}, u32[]{:S(2)}) collective-permute-start(bf16[2,6,88,256]{3,2,1,0:T(8,128)(2,1)S(1)} %get-tuple-element.10), channel_id=1, source_target_pairs={{1,0},{2,1},{3,2},{4,3},{5,4},{6,5},{7,6},{8,7},{9,8},{10,9},{11,1... | collective-permute-start | bytes 1622024 | tf_op jit(solution)/shard_map/ppermute | solution.py:247
  86.7 4.9 %collective-permute-start.1 = (bf16[2,6,88,256]{3,2,1,0:T(8,128)(2,1)S(1)}, bf16[2,6,88,256]{3,2,1,0:T(8,128)(2,1)S(1)}, u32[]{:S(2)}, u32[]{:S(2)}) collective-permute-start(bf16[2,6,88,256]{3,2,1,0:T(8,128)(2,1)S(1)} %get-tuple-element.11), channel_id=1, source_target_pairs={{0,1},{1,2},{2,3},{3,4},{4,5},{5,6},{6,7},{7,8},{8,9},{9,10},{10,1... | collective-permute-start | bytes 1622024 | tf_op jit(solution)/shard_map/ppermute | solution.py:248
  91.6 0.0 all-to-all-done.1.r_ref
  91.6 13.9 %shard_map.47.done_ref = bf16[12,6,88,256]{3,2,1,0:T(8,128)(2,1)} custom-call(s32[64,24]{1,0:T(8,128)S(1)} %get-tuple-element.32.lev, f32[6]{0:T(128)S(1)} %multiply_divide_fusion.scale, bf16[16,72,128]{2,1,0:T(8,128)(2,1)S(1)} %all-to-all-done.1.r_ref, f32[8,6,96,256]{3,2,1,0:T(8,128)} %get-tuple-element.12.p_ref, bf16[6,256,1280]{2,1,0:T(8,128)(2,1)} %fusion.1.t_ref, ...), custom_call_target="tpu_custom_call" | custom-call | flops 10000000000 | bytes 10000000 | tf_op jit(solution)/shard_map/pallas_call | solution.py:194
  105.5 0.0 collective-permute-done.right_ref
  105.5 0.0 collective-permute-done.1.left_ref
  105.5 4.7 %shard_map.48 = bf16[12,6,88,256]{3,2,1,0:T(8,128)(2,1)} custom-call(f32[6]{0:T(128)S(1)} %multiply_divide_fusion.scale, f32[4,6,88,256]{3,2,1,0:T(8,128)} %get-tuple-element.9.part_ref, bf16[2,6,88,256]{3,2,1,0:T(8,128)(2,1)S(1)} %collective-permute-done.right_ref, ...), custom_call_target="tpu_custom_call", output_to_operand_aliasing={{}: (4, {})} | custom-call | flops 1000000 | bytes 1000000 | tf_op jit(solution)/shard_map/pallas_call | solution.py:210
  (29 shorter events, 0.5 us)
Async XLA Ops:
  0.0 3.1 %copy-start = (s32[4,12,6]{1,0,2:T(4,128)S(1)}, s32[4,12,6]{1,0,2:T(4,128)}, u32[]{:S(2)}) copy-start(s32[4,12,6]{1,0,2:T(4,128)} %param.5) | copy-start | bytes 3460
  3.8 19.6 %copy-start.2 = (f32[6]{0:T(128)S(1)}, f32[6]{0:T(128)}, u32[]{:S(2)}) copy-start(f32[6]{0:T(128)} %param.7) | copy-start | bytes 76
  3.9 19.7 %copy-start.1 = (f32[6,256]{1,0:T(8,128)S(1)}, f32[6,256]{1,0:T(8,128)}, u32[]{:S(2)}) copy-start(f32[6,256]{1,0:T(8,128)} %param.6) | copy-start | bytes 18436
  5.7 41.3 %all-to-all-start = ((bf16[16,152,128]{2,1,0:T(8,128)(2,1)}), bf16[16,152,128]{2,1,0:T(8,128)(2,1)S(1)}, u32[]{:S(2)}, u32[]{:S(2)}) async-start(bf16[16,152,128]{2,1,0:T(8,128)(2,1)} %pad_maximum_fusion.1), calls=%async_computation | async-start | bytes 1245184 | tf_op jit(solution)/shard_map/all_to_all | solution.py:229
  47.0 44.7 %all-to-all-start.1 = ((bf16[16,72,128]{2,1,0:T(8,128)(2,1)}), bf16[16,72,128]{2,1,0:T(8,128)(2,1)S(1)}, u32[]{:S(2)}, u32[]{:S(2)}) async-start(bf16[16,72,128]{2,1,0:T(8,128)(2,1)} %bitcast.40), calls=%async_computation.1 | async-start | bytes 589824 | tf_op jit(solution)/shard_map/all_to_all | solution.py:229
  84.0 21.6 %collective-permute-start = (bf16[2,6,88,256]{3,2,1,0:T(8,128)(2,1)S(1)}, bf16[2,6,88,256]{3,2,1,0:T(8,128)(2,1)S(1)}, u32[]{:S(2)}, u32[]{:S(2)}) collective-permute-start(bf16[2,6,88,256]{3,2,1,0:T(8,128)(2,1)S(1)} %get-tuple-element.10), channel_id=1, source_target_pairs={{1,0},{2,1},{3,2},{4,3},{5,4},{6,5},{7,6},{8,7},{9,8},{10,9},{11,1... | collective-permute-start | bytes 1622024 | tf_op jit(solution)/shard_map/ppermute | solution.py:247
  86.7 18.8 %collective-permute-start.1 = (bf16[2,6,88,256]{3,2,1,0:T(8,128)(2,1)S(1)}, bf16[2,6,88,256]{3,2,1,0:T(8,128)(2,1)S(1)}, u32[]{:S(2)}, u32[]{:S(2)}) collective-permute-start(bf16[2,6,88,256]{3,2,1,0:T(8,128)(2,1)S(1)} %get-tuple-element.11), channel_id=1, source_target_pairs={{0,1},{1,2},{2,3},{3,4},{4,5},{5,6},{6,7},{7,8},{8,9},{9,10},{10,1... | collective-permute-start | bytes 1622024 | tf_op jit(solution)/shard_map/ppermute | solution.py:248

commit v4 on v3

--- a/solution.py
+++ b/solution.py
@@ -10,11 +10,11 @@
 F32, BF16, I32 = jnp.float32, jnp.bfloat16, jnp.int32
 SECTORS, ROWS, VARS, CELLS, BINS = 16, 12, 6, 88, 256
 WIDE = 96
+EDGE_MIB = 32
 LEVELS = 5
 FEATURES = LEVELS * 256
 GROUPS = 1
 SPLIT = 6
-JOINED = 4
 SMEM = pl.BlockSpec(memory_space=pltpu.SMEM)
 VMEM = pl.BlockSpec(memory_space=pltpu.VMEM)
 
@@ -64,7 +64,7 @@
     return ref[:, pl.ds(start, 8), :].astype(F32)
 
 
-def row_sums(chains, lev, t_ref, s_ref, word, bit, a_ref, accs, put):
+def row_sums(chains, joined, lev, t_ref, s_ref, word, bit, a_ref, accs, put):
     step = pl.program_id(0)
     part = 64 // GROUPS
     words = lax.broadcasted_iota(I32, (part, 128), 0)
@@ -81,17 +81,17 @@
                     span = pl.ds(g * part, part)
                     acc[e, span] = acc[e, span] + jnp.where(here, v, 0)
 
-    for k in range(0, 8, JOINED):
-        for c in range(k, k + JOINED):
+    for k in range(0, 8, joined):
+        for c in range(k, k + joined):
             for e in range(LEVELS):
                 a = accs[c][e]
                 accs[c][e] = jnp.zeros_like(a)
                 for j in range(4):
                     n = lax.shift_right_logical(a, 8 * j) & 255
                     a_ref[c, e * 256 + j * 64 : e * 256 + j * 64 + 64] = n.astype(F32).astype(BF16)
-        counts = jnp.concatenate([a_ref[c] for c in range(k, k + JOINED)], axis=1)
+        counts = jnp.concatenate([a_ref[c] for c in range(k, k + joined)], axis=1)
         d = jnp.dot(t_ref[chains[k][1]], counts, preferred_element_type=F32).astype(BF16)
-        for i in range(JOINED):
+        for i in range(joined):
             p = lax.dot_general(s_ref[...], d[:, i * 128 : i * 128 + 128], (((1,), (1,)), ((), ())), preferred_element_type=F32)
             put(*chains[k + i], p)
 
@@ -104,13 +104,14 @@
 
     def put(k, vv, p):
         p_ref[k, vv] = p
+        if k < 2:
+            head_ref[k, vv] = p[:CELLS].astype(BF16)
+        if k >= 6:
+            tail_ref[k - 6, vv] = p[:CELLS].astype(BF16)
 
     @pl.loop(0, 2)
     def _(vv):
-        row_sums([(k, vv) for k in range(8)], lev, t_ref, s_ref, word, bit, a_ref, accs, put)
-        for k in range(2):
-            head_ref[k, vv] = p_ref[k, vv, :CELLS].astype(BF16)
-            tail_ref[k, vv] = p_ref[6 + k, vv, :CELLS].astype(BF16)
+        row_sums([(k, vv) for k in range(8)], 8, lev, t_ref, s_ref, word, bit, a_ref, accs, put)
         low = p_ref[0, vv, :CELLS] + p_ref[1, vv, :CELLS] + p_ref[2, vv, :CELLS]
         part_ref[0, vv] = low
         part_ref[1, vv] = low + p_ref[3, vv, :CELLS]
@@ -127,7 +128,7 @@
     def put(k, vv, p):
         own[k, vv] = p
 
-    row_sums([(k, vv) for vv in range(2) for k in range(4)], lev, t_ref, s_ref, word, bit, a_ref, accs, put)
+    row_sums([(k, vv) for vv in range(2) for k in range(4)], 4, lev, t_ref, s_ref, word, bit, a_ref, accs, put)
     rows = [(p_ref, k) for k in range(4)] + [(own, k) for k in range(4)] + [(p_ref, k) for k in range(4, 8)]
 
     @pl.loop(0, 2)
@@ -141,22 +142,26 @@
             o_ref[r + 2, vv] = (total[:CELLS] * factor).astype(BF16)
 
 
-def edge_kernel(scale, part_ref, right_ref, left_ref, done_ref, o_ref):
-    end, step = pl.program_id(1), pl.program_id(0)
-    for vv in range(2):
-        factor = scale[step * 2 + vv]
-
-        @pl.when(end == 0)
-        def _():
-            last = left_ref[1, vv].astype(F32)
-            o_ref[0, vv] = ((part_ref[0, vv] + left_ref[0, vv].astype(F32) + last) * factor).astype(BF16)
-            o_ref[1, vv] = ((part_ref[1, vv] + last) * factor).astype(BF16)
-
-        @pl.when(end == 1)
-        def _():
-            next_ = right_ref[0, vv].astype(F32)
-            o_ref[0, vv] = ((part_ref[0, vv] + next_) * factor).astype(BF16)
-            o_ref[1, vv] = ((part_ref[1, vv] + next_ + right_ref[1, vv].astype(F32)) * factor).astype(BF16)
+def edge_kernel(scale, part_ref, right_ref, left_ref, done_ref, o_ref, rows, sems):
+    def copy(end):
+        return pltpu.make_async_copy(rows.at[pl.ds(2 * end, 2)], o_ref.at[pl.ds(10 * end, 2)], sems.at[end])
+
+    for end in range(2):
+
+        @pl.loop(0, VARS)
+        def _(v):
+            if end == 0:
+                near, far = left_ref[1, v].astype(F32), left_ref[0, v].astype(F32)
+                sums = part_ref[0, v] + far + near, part_ref[1, v] + near
+            else:
+                near, far = right_ref[0, v].astype(F32), right_ref[1, v].astype(F32)
+                sums = part_ref[2, v] + near, part_ref[3, v] + near + far
+            for k in range(2):
+                rows[2 * end + k, v] = (sums[k] * scale[v]).astype(BF16)
+
+        copy(end).start()
+    for end in range(2):
+        copy(end).wait()
 
 
 def scratch(slots):
@@ -204,24 +209,16 @@
 
 
 def edge_rows(scale, part, right, left, done):
-    def block(where):
-        return pl.BlockSpec((2, 2, CELLS, BINS), where)
-
+    anywhere = pl.BlockSpec(memory_space=pl.ANY)
     return pl.pallas_call(
         edge_kernel,
         out_shape=jax.ShapeDtypeStruct((ROWS, VARS, CELLS, BINS), BF16),
-        grid=(3, 2),
-        in_specs=[
-            SMEM,
-            block(lambda i, end: (end, i, 0, 0)),
-            block(lambda i, end: (0, i, 0, 0)),
-            block(lambda i, end: (0, i, 0, 0)),
-            pl.BlockSpec(memory_space=pl.ANY),
-        ],
-        out_specs=block(lambda i, end: (end * 5, i, 0, 0)),
+        in_specs=[SMEM, VMEM, VMEM, VMEM, anywhere],
+        out_specs=anywhere,
+        scratch_shapes=[pltpu.VMEM((4, VARS, CELLS, BINS), BF16), pltpu.SemaphoreType.DMA((2,))],
         input_output_aliases={4: 0},
+        compiler_params=pltpu.CompilerParams(vmem_limit_bytes=EDGE_MIB << 20),
         cost_estimate=pl.CostEstimate(flops=10**6, bytes_accessed=10**6, transcendentals=0),
-        **PARAMS,
     )(scale, part, right, left, done)
 
 

time: 111 us -> 107 us (0.964)
  Pallas kernels: 42.1 us -> 37.9 us
    pallas_call x1, Pallas kernels: 4.74 us -> 1.72 us  [edge_rows(): pl.pallas_call(edge_kernel, out_shape=jax.ShapeDtypeStruct((ROWS, VARS, C...]
    pallas_call x1, Pallas kernels: 23.5 us -> 22.2 us  [outer_rows(): pl.pallas_call(outer_kernel, out_shape=[shape(8, WIDE, F32), shape(4, CEL...]
where the time goes in v4:
time: 107 us; the launch traced here: 106 us
  Pallas kernels  37.9 us (35%)
  starting transfers between devices  35.9 us (34%)
  waiting for transfers between devices  20.2 us (19%)
  other arithmetic  7.03 us (7%)
  local copies, waits for them, and re-layouts  4.69 us (4%)
    all_to_all x2, starting transfers between devices, exchanged(): return lax.all_to_all(x, 'member', split_axis=0, concat_axis=0, tiled=True)  28.2 us
    pallas_call x1, Pallas kernels, outer_rows(): pl.pallas_call(outer_kernel, out_shape=[shape(8, WIDE, F32), shape(4, CEL...  22.2 us
    all_to_all x2, waiting for transfers between devices, exchanged(): return lax.all_to_all(x, 'member', split_axis=0, concat_axis=0, tiled=True)  20.2 us
    pallas_call x1, Pallas kernels, inner_rows(): pl.pallas_call(inner_kernel, out_shape=jax.ShapeDtypeStruct((ROWS, VARS,...  14 us
    ppermute x1, starting transfers between devices, shards(): left = lax.ppermute(tail, 'band', [(i, i + 1) for i in range(bands - 1)])  4.9 us
    convert_element_type x1, other arithmetic, kernel_table(): return jnp.exp(-0.5 * d * d).astype(BF16)  3.19 us
    ppermute x1, starting transfers between devices, shards(): right = lax.ppermute(head, 'band', [(i + 1, i) for i in range(bands - 1)])  2.76 us
  transfers between devices with their start and end apart: 4, of which 1 were waited for; matrix products, arithmetic and copies ran while one was open for 6% of the time, Pallas kernels for 34%

profile of v4, /device:TPU:7, one launch (start us, length us, event | category | flops | bytes accessed | tf_op | source)
XLA Modules:
  0.0 106.2 jit_solution(7655202081738104979)
XLA Ops:
  0.0 1.7 %convert.8 = bf16[4,12,6,1408]{3,0,2,1:T(4,128)(2,1)S(1)} convert(s32[4,12,6,1408]{3,0,2,1:T(4,128)} %param.4) | non-fusion elementwise | flops 405504 | bytes 2433024 | tf_op jit(solution)/shard_map/convert.5
  1.7 0.3 fusion.44
  2.0 0.4 pad_maximum_fusion
  2.4 0.4 fusion.15
  2.8 0.2 fusion.14
  3.1 0.0 copy-done.1
  3.1 0.1 copy.23
  3.2 0.1 reshape.132
  3.3 0.1 pad_slice_fusion.28
  3.8 0.0 copy-start.3
  3.9 0.0 copy-start.2
  4.0 0.5 reshape.130
  4.5 0.3 copy.22
  4.8 0.9 pad_maximum_fusion.1
  5.7 14.9 %all-to-all-start = ((bf16[16,152,128]{2,1,0:T(8,128)(2,1)}), bf16[16,152,128]{2,1,0:T(8,128)(2,1)S(1)}, u32[]{:S(2)}, u32[]{:S(2)}) async-start(bf16[16,152,128]{2,1,0:T(8,128)(2,1)} %pad_maximum_fusion.1), calls=%async_computation | async-start | bytes 1245184 | tf_op jit(solution)/shard_map/all_to_all | solution.py:226
  20.6 0.1 constant_dynamic-update-slice_fusion.31
  20.7 0.1 constant_dynamic-update-slice_fusion.30
  20.8 0.1 constant_dynamic-update-slice_fusion.29
  20.9 0.1 constant_dynamic-update-slice_fusion.28
  21.0 0.1 constant_dynamic-update-slice_fusion.27
  21.1 0.1 constant_dynamic-update-slice_fusion.26
  21.2 0.1 constant_dynamic-update-slice_fusion.25
  21.3 0.1 constant_dynamic-update-slice_fusion.24
  21.4 0.1 constant_dynamic-update-slice_fusion.23
  21.5 0.1 constant_dynamic-update-slice_fusion.22
  21.6 0.1 constant_dynamic-update-slice_fusion.21
  21.7 0.1 constant_dynamic-update-slice_fusion.20
  21.8 0.1 constant_dynamic-update-slice_fusion.19
  21.9 0.1 constant_dynamic-update-slice_fusion.18
  22.0 0.1 constant_dynamic-update-slice_fusion.17
  22.1 0.1 constant_dynamic-update-slice_fusion.16
  22.2 0.2 copy.24
  22.3 0.2 reshape.136
  22.6 0.8 copy.25
  23.5 0.1 fusion.20.s_ref
  23.6 3.2 %fusion.1.t_ref = bf16[6,256,1280]{2,1,0:T(8,128)(2,1)} fusion(f32[6]{0:T(128)S(1)} %copy-done.3, f32[1280]{0:T(1024)S(1)} %fusion.33, f32[6,256]{1,0:T(8,128)S(1)} %copy-done.2), kind=kLoop, calls=%fused_computation.2 | loop fusion | flops 9830400 | bytes 3943448 | tf_op jit(solution)/shard_map/convert_element_type | solution.py:45
  26.8 20.2 %all-to-all-done.r_ref = bf16[16,152,128]{2,1,0:T(8,128)(2,1)S(1)} async-done(((bf16[16,152,128]{2,1,0:T(8,128)(2,1)}), bf16[16,152,128]{2,1,0:T(8,128)(2,1)S(1)}, u32[]{:S(2)}, u32[]{:S(2)}) %all-to-all-start) | async-done | bytes 622624 | tf_op jit(solution)/shard_map/all_to_all | solution.py:226
  47.0 13.3 %all-to-all-start.1 = ((bf16[16,72,128]{2,1,0:T(8,128)(2,1)}), bf16[16,72,128]{2,1,0:T(8,128)(2,1)S(1)}, u32[]{:S(2)}, u32[]{:S(2)}) async-start(bf16[16,72,128]{2,1,0:T(8,128)(2,1)} %bitcast.40), calls=%async_computation.1 | async-start | bytes 589824 | tf_op jit(solution)/shard_map/all_to_all | solution.py:226
  60.3 0.1 fusion.45
  60.4 0.1 pad_add_fusion.lev
  60.5 22.2 %shard_map.46 = (f32[8,6,96,256]{3,2,1,0:T(8,128)}, f32[4,6,88,256]{3,2,1,0:T(8,128)}, bf16[2,6,88,256]{3,2,1,0:T(8,128)(2,1)S(1)}, bf16[2,6,88,256]{3,2,1,0:T(8,128)(2,1)S(1)}) custom-call(s32[64,48]{1,0:T(8,128)S(1)} %pad_add_fusion.lev, bf16[16,152,128]{2,1,0:T(8,128)(2,1)S(1)} %all-to-all-done.r_ref, bf16[6,256,1280]{2,1,0:T(8,128)(2,1)} %fusion.1.t_ref, ...), custom_call_target="tpu_custom_call" | custom-call | flops 10000000000 | bytes 10000000 | tf_op jit(solution)/shard_map/pallas_call | solution.py:186
  82.7 2.8 %collective-permute-start = (bf16[2,6,88,256]{3,2,1,0:T(8,128)(2,1)S(1)}, bf16[2,6,88,256]{3,2,1,0:T(8,128)(2,1)S(1)}, u32[]{:S(2)}, u32[]{:S(2)}) collective-permute-start(bf16[2,6,88,256]{3,2,1,0:T(8,128)(2,1)S(1)} %get-tuple-element.10), channel_id=1, source_target_pairs={{1,0},{2,1},{3,2},{4,3},{5,4},{6,5},{7,6},{8,7},{9,8},{10,9},{11,1... | collective-permute-start | bytes 1622024 | tf_op jit(solution)/shard_map/ppermute | solution.py:244
  85.4 4.9 %collective-permute-start.1 = (bf16[2,6,88,256]{3,2,1,0:T(8,128)(2,1)S(1)}, bf16[2,6,88,256]{3,2,1,0:T(8,128)(2,1)S(1)}, u32[]{:S(2)}, u32[]{:S(2)}) collective-permute-start(bf16[2,6,88,256]{3,2,1,0:T(8,128)(2,1)S(1)} %get-tuple-element.11), channel_id=1, source_target_pairs={{0,1},{1,2},{2,3},{3,4},{4,5},{5,6},{6,7},{7,8},{8,9},{9,10},{10,1... | collective-permute-start | bytes 1622024 | tf_op jit(solution)/shard_map/ppermute | solution.py:245
  90.4 0.0 all-to-all-done.1.r_ref
  90.4 14.0 %shard_map.47.done_ref = bf16[12,6,88,256]{3,2,1,0:T(8,128)(2,1)} custom-call(s32[64,24]{1,0:T(8,128)S(1)} %get-tuple-element.32.lev, f32[6]{0:T(128)S(1)} %multiply_divide_fusion.scale, bf16[16,72,128]{2,1,0:T(8,128)(2,1)S(1)} %all-to-all-done.1.r_ref, f32[8,6,96,256]{3,2,1,0:T(8,128)} %get-tuple-element.12.p_ref, bf16[6,256,1280]{2,1,0:T(8,128)(2,1)} %fusion.1.t_ref, ...), custom_call_target="tpu_custom_call" | custom-call | flops 10000000000 | bytes 10000000 | tf_op jit(solution)/shard_map/pallas_call | solution.py:199
  104.4 0.0 collective-permute-done.right_ref
  104.4 0.0 collective-permute-done.1.left_ref
  104.4 1.7 %shard_map.48 = bf16[12,6,88,256]{3,2,1,0:T(8,128)(2,1)} custom-call(f32[6]{0:T(128)S(1)} %multiply_divide_fusion.scale, f32[4,6,88,256]{3,2,1,0:T(8,128)S(1)} %copy-done, bf16[2,6,88,256]{3,2,1,0:T(8,128)(2,1)S(1)} %collective-permute-done.right_ref, bf16[2,6,88,256]{3,2,1,0:T(8,128)(2,1)S(1)} %collective-permute-done.1.left_ref, ...), custom_call_target="tpu_custom_call", output_to_operand_aliasing={{}: (4, {})} | custom-call | flops 1000000 | bytes 1000000 | tf_op jit(solution)/shard_map/pallas_call | solution.py:213
  (31 shorter events, 0.5 us)
Async XLA Ops:
  0.0 3.1 %copy-start.1 = (s32[4,12,6]{1,0,2:T(4,128)S(1)}, s32[4,12,6]{1,0,2:T(4,128)}, u32[]{:S(2)}) copy-start(s32[4,12,6]{1,0,2:T(4,128)} %param.5) | copy-start | bytes 3460
  3.8 19.6 %copy-start.3 = (f32[6]{0:T(128)S(1)}, f32[6]{0:T(128)}, u32[]{:S(2)}) copy-start(f32[6]{0:T(128)} %param.7) | copy-start | bytes 76
  3.9 19.7 %copy-start.2 = (f32[6,256]{1,0:T(8,128)S(1)}, f32[6,256]{1,0:T(8,128)}, u32[]{:S(2)}) copy-start(f32[6,256]{1,0:T(8,128)} %param.6) | copy-start | bytes 18436
  5.7 41.3 %all-to-all-start = ((bf16[16,152,128]{2,1,0:T(8,128)(2,1)}), bf16[16,152,128]{2,1,0:T(8,128)(2,1)S(1)}, u32[]{:S(2)}, u32[]{:S(2)}) async-start(bf16[16,152,128]{2,1,0:T(8,128)(2,1)} %pad_maximum_fusion.1), calls=%async_computation | async-start | bytes 1245184 | tf_op jit(solution)/shard_map/all_to_all | solution.py:226
  47.0 43.4 %all-to-all-start.1 = ((bf16[16,72,128]{2,1,0:T(8,128)(2,1)}), bf16[16,72,128]{2,1,0:T(8,128)(2,1)S(1)}, u32[]{:S(2)}, u32[]{:S(2)}) async-start(bf16[16,72,128]{2,1,0:T(8,128)(2,1)} %bitcast.40), calls=%async_computation.1 | async-start | bytes 589824 | tf_op jit(solution)/shard_map/all_to_all | solution.py:226
  82.7 21.7 %collective-permute-start = (bf16[2,6,88,256]{3,2,1,0:T(8,128)(2,1)S(1)}, bf16[2,6,88,256]{3,2,1,0:T(8,128)(2,1)S(1)}, u32[]{:S(2)}, u32[]{:S(2)}) collective-permute-start(bf16[2,6,88,256]{3,2,1,0:T(8,128)(2,1)S(1)} %get-tuple-element.10), channel_id=1, source_target_pairs={{1,0},{2,1},{3,2},{4,3},{5,4},{6,5},{7,6},{8,7},{9,8},{10,9},{11,1... | collective-permute-start | bytes 1622024 | tf_op jit(solution)/shard_map/ppermute | solution.py:244
  85.4 19.0 %collective-permute-start.1 = (bf16[2,6,88,256]{3,2,1,0:T(8,128)(2,1)S(1)}, bf16[2,6,88,256]{3,2,1,0:T(8,128)(2,1)S(1)}, u32[]{:S(2)}, u32[]{:S(2)}) collective-permute-start(bf16[2,6,88,256]{3,2,1,0:T(8,128)(2,1)S(1)} %get-tuple-element.11), channel_id=1, source_target_pairs={{0,1},{1,2},{2,3},{3,4},{4,5},{5,6},{6,7},{7,8},{8,9},{9,10},{10,1... | collective-permute-start | bytes 1622024 | tf_op jit(solution)/shard_map/ppermute | solution.py:245
  90.4 14.1 %copy-start = (f32[4,6,88,256]{3,2,1,0:T(8,128)S(1)}, f32[4,6,88,256]{3,2,1,0:T(8,128)}, u32[]{:S(2)}) copy-start(f32[4,6,88,256]{3,2,1,0:T(8,128)} %get-tuple-element.9.part_ref) | copy-start | bytes 6488068

commit v5 on v4

--- a/solution.py
+++ b/solution.py
@@ -69,9 +69,10 @@
     part = 64 // GROUPS
     words = lax.broadcasted_iota(I32, (part, 128), 0)
 
-    @pl.loop(0, SECTORS)
-    def _(src):
-        for mm in range(4):
+    @pl.loop(0, SECTORS // 2)
+    def _(pair):
+        for m in range(8):
+            src, mm = pair * 2 + m // 4, m % 4
             for acc, (slot, vv) in zip(accs, chains):
                 e = lev[src * 4 + mm, slot * VARS + step * 2 + vv]
                 at = pl.ds(vv * 4 + mm, 1)

time: 107 us -> 106 us (level)
  no operation moved by 1% of the time
where the time goes in v5:
time: 106 us; the launch traced here: 105 us
  Pallas kernels  37.2 us (35%)
  starting transfers between devices  35.9 us (34%)
  waiting for transfers between devices  20.2 us (19%)
  other arithmetic  7.03 us (7%)
  local copies, waits for them, and re-layouts  4.69 us (4%)
    all_to_all x2, starting transfers between devices, exchanged(): return lax.all_to_all(x, 'member', split_axis=0, concat_axis=0, tiled=True)  28.2 us
    pallas_call x1, Pallas kernels, outer_rows(): pl.pallas_call(outer_kernel, out_shape=[shape(8, WIDE, F32), shape(4, CEL...  21.7 us
    all_to_all x2, waiting for transfers between devices, exchanged(): return lax.all_to_all(x, 'member', split_axis=0, concat_axis=0, tiled=True)  20.2 us
    pallas_call x1, Pallas kernels, inner_rows(): pl.pallas_call(inner_kernel, out_shape=jax.ShapeDtypeStruct((ROWS, VARS,...  13.8 us
    ppermute x1, starting transfers between devices, shards(): left = lax.ppermute(tail, 'band', [(i, i + 1) for i in range(bands - 1)])  4.92 us
    convert_element_type x1, other arithmetic, kernel_table(): return jnp.exp(-0.5 * d * d).astype(BF16)  3.19 us
    ppermute x1, starting transfers between devices, shards(): right = lax.ppermute(head, 'band', [(i + 1, i) for i in range(bands - 1)])  2.74 us
  transfers between devices with their start and end apart: 4, of which 1 were waited for; matrix products, arithmetic and copies ran while one was open for 6% of the time, Pallas kernels for 34%

profile of v5, /device:TPU:7, one launch (start us, length us, event | category | flops | bytes accessed | tf_op | source)
XLA Modules:
  0.0 105.4 jit_solution(2311819584019198562)
XLA Ops:
  0.0 1.7 %convert.8 = bf16[4,12,6,1408]{3,0,2,1:T(4,128)(2,1)S(1)} convert(s32[4,12,6,1408]{3,0,2,1:T(4,128)} %param.4) | non-fusion elementwise | flops 405504 | bytes 2433024 | tf_op jit(solution)/shard_map/convert.5
  1.7 0.3 fusion.44
  2.0 0.4 pad_maximum_fusion
  2.4 0.4 fusion.15
  2.8 0.2 fusion.14
  3.1 0.0 copy-done.1
  3.1 0.1 copy.23
  3.2 0.1 reshape.132
  3.3 0.1 pad_slice_fusion.28
  3.8 0.0 copy-start.3
  3.9 0.0 copy-start.2
  4.0 0.5 reshape.130
  4.5 0.3 copy.22
  4.8 0.9 pad_maximum_fusion.1
  5.7 14.9 %all-to-all-start = ((bf16[16,152,128]{2,1,0:T(8,128)(2,1)}), bf16[16,152,128]{2,1,0:T(8,128)(2,1)S(1)}, u32[]{:S(2)}, u32[]{:S(2)}) async-start(bf16[16,152,128]{2,1,0:T(8,128)(2,1)} %pad_maximum_fusion.1), calls=%async_computation | async-start | bytes 1245184 | tf_op jit(solution)/shard_map/all_to_all | solution.py:227
  20.6 0.1 constant_dynamic-update-slice_fusion.31
  20.7 0.1 constant_dynamic-update-slice_fusion.30
  20.8 0.1 constant_dynamic-update-slice_fusion.29
  20.9 0.1 constant_dynamic-update-slice_fusion.28
  21.0 0.1 constant_dynamic-update-slice_fusion.27
  21.1 0.1 constant_dynamic-update-slice_fusion.26
  21.2 0.1 constant_dynamic-update-slice_fusion.25
  21.3 0.1 constant_dynamic-update-slice_fusion.24
  21.4 0.1 constant_dynamic-update-slice_fusion.23
  21.5 0.1 constant_dynamic-update-slice_fusion.22
  21.6 0.1 constant_dynamic-update-slice_fusion.21
  21.7 0.1 constant_dynamic-update-slice_fusion.20
  21.8 0.1 constant_dynamic-update-slice_fusion.19
  21.9 0.1 constant_dynamic-update-slice_fusion.18
  22.0 0.1 constant_dynamic-update-slice_fusion.17
  22.1 0.1 constant_dynamic-update-slice_fusion.16
  22.2 0.2 copy.24
  22.3 0.2 reshape.136
  22.6 0.8 copy.25
  23.5 0.1 fusion.20.s_ref
  23.6 3.2 %fusion.1.t_ref = bf16[6,256,1280]{2,1,0:T(8,128)(2,1)} fusion(f32[6]{0:T(128)S(1)} %copy-done.3, f32[1280]{0:T(1024)S(1)} %fusion.33, f32[6,256]{1,0:T(8,128)S(1)} %copy-done.2), kind=kLoop, calls=%fused_computation.2 | loop fusion | flops 9830400 | bytes 3943448 | tf_op jit(solution)/shard_map/convert_element_type | solution.py:45
  26.8 20.2 %all-to-all-done.r_ref = bf16[16,152,128]{2,1,0:T(8,128)(2,1)S(1)} async-done(((bf16[16,152,128]{2,1,0:T(8,128)(2,1)}), bf16[16,152,128]{2,1,0:T(8,128)(2,1)S(1)}, u32[]{:S(2)}, u32[]{:S(2)}) %all-to-all-start) | async-done | bytes 622624 | tf_op jit(solution)/shard_map/all_to_all | solution.py:227
  47.0 13.3 %all-to-all-start.1 = ((bf16[16,72,128]{2,1,0:T(8,128)(2,1)}), bf16[16,72,128]{2,1,0:T(8,128)(2,1)S(1)}, u32[]{:S(2)}, u32[]{:S(2)}) async-start(bf16[16,72,128]{2,1,0:T(8,128)(2,1)} %bitcast.40), calls=%async_computation.1 | async-start | bytes 589824 | tf_op jit(solution)/shard_map/all_to_all | solution.py:227
  60.3 0.1 fusion.45
  60.4 0.1 pad_add_fusion.lev
  60.5 21.7 %shard_map.46 = (f32[8,6,96,256]{3,2,1,0:T(8,128)}, f32[4,6,88,256]{3,2,1,0:T(8,128)}, bf16[2,6,88,256]{3,2,1,0:T(8,128)(2,1)S(1)}, bf16[2,6,88,256]{3,2,1,0:T(8,128)(2,1)S(1)}) custom-call(s32[64,48]{1,0:T(8,128)S(1)} %pad_add_fusion.lev, bf16[16,152,128]{2,1,0:T(8,128)(2,1)S(1)} %all-to-all-done.r_ref, bf16[6,256,1280]{2,1,0:T(8,128)(2,1)} %fusion.1.t_ref, ...), custom_call_target="tpu_custom_call" | custom-call | flops 10000000000 | bytes 10000000 | tf_op jit(solution)/shard_map/pallas_call | solution.py:187
  82.2 2.7 %collective-permute-start = (bf16[2,6,88,256]{3,2,1,0:T(8,128)(2,1)S(1)}, bf16[2,6,88,256]{3,2,1,0:T(8,128)(2,1)S(1)}, u32[]{:S(2)}, u32[]{:S(2)}) collective-permute-start(bf16[2,6,88,256]{3,2,1,0:T(8,128)(2,1)S(1)} %get-tuple-element.10), channel_id=1, source_target_pairs={{1,0},{2,1},{3,2},{4,3},{5,4},{6,5},{7,6},{8,7},{9,8},{10,9},{11,1... | collective-permute-start | bytes 1622024 | tf_op jit(solution)/shard_map/ppermute | solution.py:245
  84.9 4.9 %collective-permute-start.1 = (bf16[2,6,88,256]{3,2,1,0:T(8,128)(2,1)S(1)}, bf16[2,6,88,256]{3,2,1,0:T(8,128)(2,1)S(1)}, u32[]{:S(2)}, u32[]{:S(2)}) collective-permute-start(bf16[2,6,88,256]{3,2,1,0:T(8,128)(2,1)S(1)} %get-tuple-element.11), channel_id=1, source_target_pairs={{0,1},{1,2},{2,3},{3,4},{4,5},{5,6},{6,7},{7,8},{8,9},{9,10},{10,1... | collective-permute-start | bytes 1622024 | tf_op jit(solution)/shard_map/ppermute | solution.py:246
  89.8 0.0 all-to-all-done.1.r_ref
  89.9 13.8 %shard_map.47.done_ref = bf16[12,6,88,256]{3,2,1,0:T(8,128)(2,1)} custom-call(s32[64,24]{1,0:T(8,128)S(1)} %get-tuple-element.32.lev, f32[6]{0:T(128)S(1)} %multiply_divide_fusion.scale, bf16[16,72,128]{2,1,0:T(8,128)(2,1)S(1)} %all-to-all-done.1.r_ref, f32[8,6,96,256]{3,2,1,0:T(8,128)} %get-tuple-element.12.p_ref, bf16[6,256,1280]{2,1,0:T(8,128)(2,1)} %fusion.1.t_ref, ...), custom_call_target="tpu_custom_call" | custom-call | flops 10000000000 | bytes 10000000 | tf_op jit(solution)/shard_map/pallas_call | solution.py:200
  103.7 0.0 collective-permute-done.right_ref
  103.7 0.0 collective-permute-done.1.left_ref
  103.7 1.7 %shard_map.48 = bf16[12,6,88,256]{3,2,1,0:T(8,128)(2,1)} custom-call(f32[6]{0:T(128)S(1)} %multiply_divide_fusion.scale, f32[4,6,88,256]{3,2,1,0:T(8,128)S(1)} %copy-done, bf16[2,6,88,256]{3,2,1,0:T(8,128)(2,1)S(1)} %collective-permute-done.right_ref, bf16[2,6,88,256]{3,2,1,0:T(8,128)(2,1)S(1)} %collective-permute-done.1.left_ref, ...), custom_call_target="tpu_custom_call", output_to_operand_aliasing={{}: (4, {})} | custom-call | flops 1000000 | bytes 1000000 | tf_op jit(solution)/shard_map/pallas_call | solution.py:214
  (31 shorter events, 0.5 us)
Async XLA Ops:
  0.0 3.1 %copy-start.1 = (s32[4,12,6]{1,0,2:T(4,128)S(1)}, s32[4,12,6]{1,0,2:T(4,128)}, u32[]{:S(2)}) copy-start(s32[4,12,6]{1,0,2:T(4,128)} %param.5) | copy-start | bytes 3460
  3.8 19.6 %copy-start.3 = (f32[6]{0:T(128)S(1)}, f32[6]{0:T(128)}, u32[]{:S(2)}) copy-start(f32[6]{0:T(128)} %param.7) | copy-start | bytes 76
  3.9 19.7 %copy-start.2 = (f32[6,256]{1,0:T(8,128)S(1)}, f32[6,256]{1,0:T(8,128)}, u32[]{:S(2)}) copy-start(f32[6,256]{1,0:T(8,128)} %param.6) | copy-start | bytes 18436
  5.7 41.3 %all-to-all-start = ((bf16[16,152,128]{2,1,0:T(8,128)(2,1)}), bf16[16,152,128]{2,1,0:T(8,128)(2,1)S(1)}, u32[]{:S(2)}, u32[]{:S(2)}) async-start(bf16[16,152,128]{2,1,0:T(8,128)(2,1)} %pad_maximum_fusion.1), calls=%async_computation | async-start | bytes 1245184 | tf_op jit(solution)/shard_map/all_to_all | solution.py:227
  47.0 42.9 %all-to-all-start.1 = ((bf16[16,72,128]{2,1,0:T(8,128)(2,1)}), bf16[16,72,128]{2,1,0:T(8,128)(2,1)S(1)}, u32[]{:S(2)}, u32[]{:S(2)}) async-start(bf16[16,72,128]{2,1,0:T(8,128)(2,1)} %bitcast.40), calls=%async_computation.1 | async-start | bytes 589824 | tf_op jit(solution)/shard_map/all_to_all | solution.py:227
  82.2 21.5 %collective-permute-start = (bf16[2,6,88,256]{3,2,1,0:T(8,128)(2,1)S(1)}, bf16[2,6,88,256]{3,2,1,0:T(8,128)(2,1)S(1)}, u32[]{:S(2)}, u32[]{:S(2)}) collective-permute-start(bf16[2,6,88,256]{3,2,1,0:T(8,128)(2,1)S(1)} %get-tuple-element.10), channel_id=1, source_target_pairs={{1,0},{2,1},{3,2},{4,3},{5,4},{6,5},{7,6},{8,7},{9,8},{10,9},{11,1... | collective-permute-start | bytes 1622024 | tf_op jit(solution)/shard_map/ppermute | solution.py:245
  84.9 18.8 %collective-permute-start.1 = (bf16[2,6,88,256]{3,2,1,0:T(8,128)(2,1)S(1)}, bf16[2,6,88,256]{3,2,1,0:T(8,128)(2,1)S(1)}, u32[]{:S(2)}, u32[]{:S(2)}) collective-permute-start(bf16[2,6,88,256]{3,2,1,0:T(8,128)(2,1)S(1)} %get-tuple-element.11), channel_id=1, source_target_pairs={{0,1},{1,2},{2,3},{3,4},{4,5},{5,6},{6,7},{7,8},{8,9},{9,10},{10,1... | collective-permute-start | bytes 1622024 | tf_op jit(solution)/shard_map/ppermute | solution.py:246
  89.8 13.8 %copy-start = (f32[4,6,88,256]{3,2,1,0:T(8,128)S(1)}, f32[4,6,88,256]{3,2,1,0:T(8,128)}, u32[]{:S(2)}) copy-start(f32[4,6,88,256]{3,2,1,0:T(8,128)} %get-tuple-element.9.part_ref) | copy-start | bytes 6488068
